TPU v7x, 512 devices: a whole 4x8x8 slice. The times are simulated.
512 devices in a mesh: gx: 8 (over z), gy: 8 (over x, y_lo), gz: 8 (over y_hi, core).
Axes of the slice: x: 4, y: 8 (y_hi: 4, y_lo: 2; y = y_hi * 2 + y_lo), z: 8, core: 2. Of those that a mesh axis runs over, the one named last changes fastest.
Arguments:
- inputs: bfloat16 [512, 12288], P(('gx', 'gy'), 'gz'), may hold values from -6 to 6
- out_grad: bfloat16 [512, 12288], P(('gx', 'gy'), 'gz'), may hold values from -6 to 6
- preact: bfloat16 [512, 24576], P('gz', ('gx', 'gy')), may hold values from -6 to 6
- w_in: bfloat16 [12288, 24576], P('gz', ('gx', 'gy')), may hold values from -0.0546875 to 0.0546875
- w_out: bfloat16 [24576, 12288], P(('gx', 'gy'), 'gz'), may hold values from -0.0390625 to 0.0390625
Outputs:
- grad_input: bfloat16 [512, 12288], P(('gx', 'gy'), 'gz')
- grad_w_in: bfloat16 [12288, 24576], P('gz', ('gx', 'gy'))
- grad_w_out: bfloat16 [24576, 12288], P(('gx', 'gy'), 'gz')
All inputs are finite; a program needn't handle non-finite values.
Results may differ from a plain program's by a relative error of at most 0.0049.
Values may be sent and summed in bfloat16 or wider, within the bound.
No kernel may reach another device: no remote copies, remote signals or barrier semaphores. Data moves between devices by JAX's collectives and lax.ppermute only.
A program may use at most 64 MiB of HBM per device.

v0:
```python
import jax
import jax.numpy as jnp
from jax import lax
from jax.sharding import PartitionSpec as P

gelu_scale = 0.7978845608028654
cubic_coef = 0.044715


def gelu_parts(pre_float):
    tanh_arg = gelu_scale * (pre_float + cubic_coef * pre_float * pre_float * pre_float)
    tangent = jnp.tanh(tanh_arg)
    value = 0.5 * pre_float * (1.0 + tangent)
    slope = 0.5 * (1.0 + tangent) + 0.5 * pre_float * (1.0 - tangent * tangent) * gelu_scale * (
        1.0 + 3.0 * cubic_coef * pre_float * pre_float
    )
    return (value, slope)


def contract_rows(left, right):
    return lax.dot_general(
        left, right, (((1,), (1,)), ((), ())), preferred_element_type=jnp.float32
    )


def contract_cols(left, right):
    return lax.dot_general(
        left, right, (((0,), (0,)), ((), ())), preferred_element_type=jnp.float32
    )


def on_device(inputs, out_grad, preact, w_in, w_out):
    rows_x, rows_dy = (
        lax.all_gather(inputs, ("gx", "gy"), axis=0, tiled=True),
        lax.all_gather(out_grad, ("gx", "gy"), axis=0, tiled=True),
    )
    picked = rows_dy
    grad_hidden = lax.psum_scatter(
        contract_rows(picked, w_out), "gz", scatter_dimension=0, tiled=True
    )
    value_local, slope_local = gelu_parts(preact.astype(jnp.float32))
    grad_pre = (grad_hidden * slope_local).astype(jnp.bfloat16)
    hidden_local = value_local.astype(jnp.bfloat16)
    grad_all, hidden_all = (
        lax.all_gather(grad_pre, "gz", axis=0, tiled=True),
        lax.all_gather(hidden_local, "gz", axis=0, tiled=True),
    )
    grad_w_out = contract_cols(hidden_all, rows_dy).astype(jnp.bfloat16)
    grad_w_in = contract_cols(rows_x, grad_all).astype(jnp.bfloat16)
    picked = grad_all
    grad_input = lax.psum_scatter(
        contract_rows(picked, w_in), ("gx", "gy"), scatter_dimension=0, tiled=True
    ).astype(jnp.bfloat16)
    return (grad_input, grad_w_in, grad_w_out)


def solution(mesh):
    in_specs = (
        P(("gx", "gy"), "gz"),
        P(("gx", "gy"), "gz"),
        P("gz", ("gx", "gy")),
        P("gz", ("gx", "gy")),
        P(("gx", "gy"), "gz"),
    )
    out_specs = (P(("gx", "gy"), "gz"), P("gz", ("gx", "gy")), P(("gx", "gy"), "gz"))
    return jax.shard_map(
        on_device, mesh=mesh, in_specs=in_specs, out_specs=out_specs, check_vma=False
    )
```

profile of v0, /device:TPU:16, one launch (start us, length us, event | category | flops | bytes accessed | tf_op | source)
XLA Modules:
  0.0 995.1 jit_solution(596862571673999329)
XLA Ops:
  7.2 0.0 copy-start
  7.2 0.0 all-gather.3.cloned.1.call-start
  7.2 0.7 all-gather.3.cloned.1.call-update
  7.9 0.0 copy-start.1
  7.9 0.0 reduce-scatter.3.cloned.1.call-start
  8.0 309.0 %all-gather.3.cloned.1.call-done = bf16[512,1536]{1,0:T(8,128)(2,1)} async-done(((bf16[8,1536]{1,0:T(8,128)(2,1)}), bf16[512,1536]{1,0:T(8,128)(2,1)}) %all-gather.3.cloned.1.call-update) | async-done | bytes 1572880 | tf_op jit(solution)/shard_map/all_gather | solution.py:35
  317.0 3.6 fusion.12
  320.6 0.0 reduce-scatter.3.cloned.1.call-update
  320.6 0.0 all-gather.5.cloned.1.call-start
  320.7 0.7 all-gather.5.cloned.1.call-update
  321.4 0.0 reduce-scatter.5.cloned.1.call-start
  321.4 32.7 %reduce-scatter.3.cloned.1.call-done = f32[64,384]{1,0:T(8,128)} async-done(((f32[512,384]{1,0:T(8,128)}), f32[64,384]{1,0:T(8,128)}) %reduce-scatter.3.cloned.1.call-update) | async-done | bytes 98320 | tf_op jit(solution)/shard_map/reduce_scatter | solution.py:38
  354.1 0.0 copy-done.1
  354.1 1.0 fusion.8
  355.1 16.7 %all_gather.13 = bf16[512,384]{1,0:T(8,128)(2,1)S(1)} all-gather(bf16[64,384]{1,0:T(8,128)(2,1)S(1)} %get-tuple-element.7), channel_id=1, replica_groups=mesh['gx'=8,'gy'=8,'gz'=8] {'gz'}, dimensions={0}, use_global_device_ids=true | all-gather | bytes 442368 | tf_op jit(solution)/shard_map/all_gather | solution.py:45
  371.8 2.6 fusion.13
  374.4 0.0 reduce-scatter.5.cloned.1.call-update
  374.4 287.2 %all-gather.5.cloned.1.call-done = bf16[512,1536]{1,0:T(8,128)(2,1)} async-done(((bf16[8,1536]{1,0:T(8,128)(2,1)}), bf16[512,1536]{1,0:T(8,128)(2,1)}) %all-gather.5.cloned.1.call-update) | async-done | bytes 1572880 | tf_op jit(solution)/shard_map/all_gather | solution.py:34
  661.6 2.2 fusion
  663.8 1.4 copy.8
  665.2 15.2 %all_gather.15 = bf16[512,384]{1,0:T(8,128)(2,1)S(1)} all-gather(bf16[64,384]{1,0:T(8,128)(2,1)S(1)} %get-tuple-element.6), channel_id=1, replica_groups=mesh['gx'=8,'gy'=8,'gz'=8] {'gz'}, dimensions={0}, use_global_device_ids=true | all-gather | bytes 442368 | tf_op jit(solution)/shard_map/all_gather | solution.py:46
  680.4 3.2 convolution_convert_fusion
  683.6 303.5 %reduce-scatter.5.cloned.1.call-done = f32[8,1536]{1,0:T(8,128)} async-done(((f32[512,1536]{1,0:T(8,128)}), f32[8,1536]{1,0:T(8,128)}) %reduce-scatter.5.cloned.1.call-update) | async-done | bytes 49168 | tf_op jit(solution)/shard_map/reduce_scatter | solution.py:51
  987.2 1.4 convert_element_type.23
  (1 shorter events, 0.0 us)
Async XLA Ops:
  7.2 364.6 %copy-start = (bf16[1536,384]{1,0:T(8,128)(2,1)S(1)}, bf16[1536,384]{1,0:T(8,128)(2,1)}, u32[]{:S(2)}) copy-start(bf16[1536,384]{1,0:T(8,128)(2,1)} %param.8) | copy-start | bytes 3538948
  7.2 309.8 %all-gather.3.cloned.1.call-start = ((), (), s32[]{:S(2)}) async-start(), calls=%async_computation.2 | async-start | bytes 1597440 | tf_op jit(solution)/shard_map/all_gather | solution.py:35
  7.9 346.2 %copy-start.1 = (bf16[64,384]{1,0:T(8,128)(2,1)S(1)}, bf16[64,384]{1,0:T(8,128)(2,1)}, u32[]{:S(2)}) copy-start(bf16[64,384]{1,0:T(8,128)(2,1)} %param.7) | copy-start | bytes 147460
  7.9 346.2 %reduce-scatter.3.cloned.1.call-start = ((), (), s32[]{:S(2)}) async-start(), calls=%async_computation.3 | async-start | bytes 884736 | tf_op jit(solution)/shard_map/reduce_scatter | solution.py:38
  320.6 341.0 %all-gather.5.cloned.1.call-start = ((), (), s32[]{:S(2)}) async-start(), calls=%async_computation.5 | async-start | bytes 1597440 | tf_op jit(solution)/shard_map/all_gather | solution.py:34
  321.4 665.8 %reduce-scatter.5.cloned.1.call-start = ((), (), s32[]{:S(2)}) async-start(), calls=%async_computation.4 | async-start | bytes 3194880 | tf_op jit(solution)/shard_map/reduce_scatter | solution.py:51
Sparse Core Ops, SparseCore 0:
  10.1 306.8 all-gather.2
  320.8 33.3 reduce-scatter.2
  356.4 305.1 all-gather.4
  664.5 322.6 reduce-scatter.4
where the time goes:
time: 995 us
  waiting for transfers between devices  934 us (94%)
  blocking collectives  31.8 us (3%)
  between operations  13.8 us (1%)
  matrix products  11.7 us (1%)
    all_gather x1, waiting for transfers between devices, on_device(): lax.all_gather(out_grad, ('gx', 'gy'), axis=0, tiled=True)  309 us
    reduce_scatter x1, waiting for transfers between devices, on_device(): lax.psum_scatter(contract_rows(picked, w_in), ('gx', 'gy'), scatter_dimen...  304 us
    all_gather x1, waiting for transfers between devices, on_device(): lax.all_gather(inputs, ('gx', 'gy'), axis=0, tiled=True)  287 us
    reduce_scatter x1, waiting for transfers between devices, on_device(): lax.psum_scatter(contract_rows(picked, w_out), 'gz', scatter_dimension=0,...  32.7 us
  transfers between devices with their start and end apart: 4, of which 4 were waited for; matrix products, arithmetic and copies ran while one was open for 1% of the time, Pallas kernels for 0%

commit v1 on v0

v1 whole, which is shorter than its diff:
```python
import jax
import jax.numpy as jnp
from jax import lax
from jax.sharding import PartitionSpec as P

gelu_scale = 0.7978845608028654
cubic_coef = 0.044715


def gelu_parts(pre_float):
    tanh_arg = gelu_scale * (pre_float + cubic_coef * pre_float * pre_float * pre_float)
    tangent = jnp.tanh(tanh_arg)
    value = 0.5 * pre_float * (1.0 + tangent)
    slope = 0.5 * (1.0 + tangent) + 0.5 * pre_float * (1.0 - tangent * tangent) * gelu_scale * (
        1.0 + 3.0 * cubic_coef * pre_float * pre_float
    )
    return (value, slope)


def contract_rows(left, right):
    return lax.dot_general(
        left, right, (((1,), (1,)), ((), ())), preferred_element_type=jnp.float32
    )


def contract_cols(left, right):
    return lax.dot_general(
        left, right, (((0,), (0,)), ((), ())), preferred_element_type=jnp.float32
    )


def swap(blocks, axis):
    return lax.all_to_all(blocks, axis, split_axis=0, concat_axis=0, tiled=True)


def gather(block, axis, size):
    return swap(jnp.broadcast_to(block[None], (size,) + block.shape), axis)


def make(sizes):
    nx, ny, nz = sizes

    def on_device(inputs, out_grad, preact, w_in, w_out):
        tokens, width = inputs.shape
        rows_z, hidden_width = preact.shape
        total = nx * ny * tokens
        both = gather(jnp.stack([inputs, out_grad]), "gx", nx)
        rows_dy = gather(both[:, 1], "gy", ny).reshape(total, width)
        rows_x = gather(both[:, 0], "gy", ny).reshape(total, width)

        partial = contract_rows(rows_dy, w_out).astype(jnp.bfloat16)
        partial = partial.reshape(ny, nx, tokens, hidden_width).transpose(1, 0, 2, 3)
        partial = swap(partial.reshape(nz, rows_z, hidden_width), "gz")
        grad_hidden = jnp.sum(partial.astype(jnp.float32), axis=0)

        value_local, slope_local = gelu_parts(preact.astype(jnp.float32))
        grad_pre = (grad_hidden * slope_local).astype(jnp.bfloat16)
        hidden_local = value_local.astype(jnp.bfloat16)
        pair = gather(jnp.stack([grad_pre, hidden_local]), "gz", nz)

        def by_gy(block):
            block = block.reshape(nx, ny, tokens, hidden_width)
            return block.transpose(1, 0, 2, 3).reshape(total, hidden_width)

        grad_all, hidden_all = by_gy(pair[:, 0]), by_gy(pair[:, 1])

        part_in = contract_rows(grad_all, w_in).astype(jnp.bfloat16)
        part_in = swap(part_in.reshape(ny, nx * tokens, width), "gy")
        part_in = jnp.sum(part_in.astype(jnp.float32), axis=0).astype(jnp.bfloat16)
        part_in = swap(part_in.reshape(nx, tokens, width), "gx")
        grad_input = jnp.sum(part_in.astype(jnp.float32), axis=0).astype(jnp.bfloat16)

        grad_w_out = contract_cols(hidden_all, rows_dy).astype(jnp.bfloat16)
        grad_w_in = contract_cols(rows_x, grad_all).astype(jnp.bfloat16)
        return (grad_input, grad_w_in, grad_w_out)

    return on_device


def solution(mesh):
    in_specs = (
        P(("gx", "gy"), "gz"),
        P(("gx", "gy"), "gz"),
        P("gz", ("gx", "gy")),
        P("gz", ("gx", "gy")),
        P(("gx", "gy"), "gz"),
    )
    out_specs = (P(("gx", "gy"), "gz"), P("gz", ("gx", "gy")), P(("gx", "gy"), "gz"))
    sizes = tuple(mesh.shape[a] for a in ("gx", "gy", "gz"))
    return jax.shard_map(
        make(sizes), mesh=mesh, in_specs=in_specs, out_specs=out_specs, check_vma=False
    )
```

time: 995 us -> 164 us (0.16)
  the two profiles are of different devices: /device:TPU:16 before, /device:TPU:10 now
where the time goes in v1:
time: 164 us
  blocking collectives  95.6 us (58%)
  waiting for transfers between devices  36.7 us (22%)
  starting transfers between devices  13.8 us (8%)
  matrix products  9.85 us (6%)
  local copies, waits for them, and re-layouts  4.56 us (3%)
  other arithmetic  2.58 us (2%)
    all_to_all x4, blocking collectives, swap(): return lax.all_to_all(blocks, axis, split_axis=0, concat_axis=0, tiled=True)  95.6 us
    all_to_all x3, waiting for transfers between devices, swap(): return lax.all_to_all(blocks, axis, split_axis=0, concat_axis=0, tiled=True)  36.7 us
    all_to_all x3, starting transfers between devices, swap(): return lax.all_to_all(blocks, axis, split_axis=0, concat_axis=0, tiled=True)  13.8 us
    dot_general x2, matrix products, contract_cols(): lax.dot_general(left, right, (((0,), (0,)), ((), ())), preferred_element_...  6.69 us
  transfers between devices with their start and end apart: 3, of which 3 were waited for; matrix products, arithmetic and copies ran while one was open for 6% of the time, Pallas kernels for 0%

profile of v1, /device:TPU:10, one launch (start us, length us, event | category | flops | bytes accessed | tf_op | source)
XLA Modules:
  0.0 163.8 jit_solution(2442445173232849136)
XLA Ops:
  0.6 0.9 pad_maximum_fusion.1
  1.5 24.8 %all_to_all.35 = bf16[8,2,8,1536]{3,2,1,0:T(8,128)(2,1)S(1)} all-to-all(bf16[8,2,8,1536]{3,2,1,0:T(8,128)(2,1)S(1)} %broadcast_in_dim.12), channel_id=1, replica_groups=mesh['gx'=8,'gy'=8,'gz'=8] {'gx'}, dimensions={0} | all-to-all | bytes 786432 | tf_op jit(solution)/shard_map/all_to_all | solution.py:33
  26.4 0.1 broadcast_in_dim.28
  26.5 23.5 %all_to_all.36 = bf16[8,8,8,1536]{3,2,1,0:T(8,128)(2,1)S(1)} all-to-all(bf16[8,8,8,1536]{3,2,1,0:T(8,128)(2,1)S(1)} %broadcast_in_dim.28), channel_id=1, replica_groups=mesh['gx'=8,'gy'=8,'gz'=8] {'gy'}, dimensions={0} | all-to-all | bytes 3145728 | tf_op jit(solution)/shard_map/all_to_all | solution.py:33
  50.0 1.0 convolution_convert_fusion.1
  51.0 0.1 copy-done.1
  51.2 21.1 %all_to_all.37 = bf16[8,64,384]{2,1,0:T(8,128)(2,1)S(1)} all-to-all(bf16[8,64,384]{2,1,0:T(8,128)(2,1)S(1)} %bitcast.54), channel_id=1, replica_groups=mesh['gx'=8,'gy'=8,'gz'=8] {'gz'}, dimensions={0} | all-to-all | bytes 786432 | tf_op jit(solution)/shard_map/all_to_all | solution.py:33
  72.5 0.1 broadcast_in_dim.29
  72.6 26.2 %all_to_all.38 = bf16[8,2,64,384]{3,2,1,0:T(8,128)(2,1)S(1)} all-to-all(bf16[8,2,64,384]{3,2,1,0:T(8,128)(2,1)S(1)} %broadcast_in_dim.29), channel_id=1, replica_groups=mesh['gx'=8,'gy'=8,'gz'=8] {'gz'}, dimensions={0} | all-to-all | bytes 1572864 | tf_op jit(solution)/shard_map/all_to_all | solution.py:33
  98.8 1.3 broadcast_in_dim.31
  100.1 4.8 %all-to-all-start.6 = ((bf16[8,8,8,1536]{3,2,1,0:T(8,128)(2,1)}), bf16[8,8,8,1536]{3,2,1,0:T(8,128)(2,1)S(1)}, u32[]{:S(2)}, u32[]{:S(2)}) async-start(bf16[8,8,8,1536]{3,2,1,0:T(8,128)(2,1)} %broadcast_in_dim.31), calls=%async_computation.6 | async-start | bytes 3145728 | tf_op jit(solution)/shard_map/all_to_all | solution.py:33
  104.9 0.8 slice_bitcast_fusion
  105.8 0.7 copy-done.3
  106.6 2.2 %convolution_convert_fusion = bf16[512,1536]{1,0:T(8,128)(2,1)} fusion(bf16[512,384]{1,0:T(8,128)(2,1)S(1)} %bitcast.55, bf16[1536,384]{1,0:T(8,128)(2,1)S(1)} %copy-done), kind=kOutput, calls=%fused_computation.2 | convolution fusion | flops 604766208 | bytes 3145728 | tf_op jit(solution)/shard_map/dot_general | solution.py:21
  108.7 14.4 %all-to-all-done.6 = bf16[8,8,8,1536]{3,2,1,0:T(8,128)(2,1)S(1)} async-done(((bf16[8,8,8,1536]{3,2,1,0:T(8,128)(2,1)}), bf16[8,8,8,1536]{3,2,1,0:T(8,128)(2,1)S(1)}, u32[]{:S(2)}, u32[]{:S(2)}) %all-to-all-start.6) | async-done | bytes 1572896 | tf_op jit(solution)/shard_map/all_to_all | solution.py:33
  123.1 1.2 copy-done.2
  124.3 5.6 %all-to-all-start.4 = ((bf16[8,64,1536]{2,1,0:T(8,128)(2,1)}), bf16[8,64,1536]{2,1,0:T(8,128)(2,1)S(1)}, u32[]{:S(2)}, u32[]{:S(2)}) async-start(bf16[8,64,1536]{2,1,0:T(8,128)(2,1)} %bitcast.12), calls=%async_computation.4 | async-start | bytes 3145728 | tf_op jit(solution)/shard_map/all_to_all | solution.py:33
  129.8 3.5 %fusion = bf16[1536,384]{1,0:T(8,128)(2,1)} fusion(bf16[8,8,8,1536]{3,2,1,0:T(8,128)(2,1)} %copy-done.2, bf16[8,8,8,384]{3,2,1,0:T(8,128)(2,1)S(1)} %copy-done.4), kind=kOutput, calls=%fused_computation.3 | convolution fusion | flops 604569600 | bytes 3145728 | tf_op jit(solution)/shard_map/dot_general | solution.py:27
  133.3 14.9 %all-to-all-done.4 = bf16[8,64,1536]{2,1,0:T(8,128)(2,1)S(1)} async-done(((bf16[8,64,1536]{2,1,0:T(8,128)(2,1)}), bf16[8,64,1536]{2,1,0:T(8,128)(2,1)S(1)}, u32[]{:S(2)}, u32[]{:S(2)}) %all-to-all-start.4) | async-done | bytes 1572896 | tf_op jit(solution)/shard_map/all_to_all | solution.py:33
  148.1 0.9 reduce_sum.34
  149.1 3.4 %all-to-all-start.5 = ((bf16[8,8,1536]{2,1,0:T(8,128)(2,1)}), bf16[8,8,1536]{2,1,0:T(8,128)(2,1)S(1)}, u32[]{:S(2)}, u32[]{:S(2)}) async-start(bf16[8,8,1536]{2,1,0:T(8,128)(2,1)} %bitcast.13), calls=%async_computation.5 | async-start | bytes 393216 | tf_op jit(solution)/shard_map/all_to_all | solution.py:33
  152.5 3.2 %fusion.1 = bf16[384,1536]{1,0:T(8,128)(2,1)} fusion(bf16[8,8,8,1536]{3,2,1,0:T(8,128)(2,1)} %copy-done.1, bf16[8,8,8,384]{3,2,1,0:T(8,128)(2,1)S(1)} %copy-done.5), kind=kOutput, calls=%fused_computation.4 | convolution fusion | flops 604569600 | bytes 3145728 | tf_op jit(solution)/shard_map/dot_general | solution.py:27
  155.7 7.4 %all-to-all-done.5 = bf16[8,8,1536]{2,1,0:T(8,128)(2,1)S(1)} async-done(((bf16[8,8,1536]{2,1,0:T(8,128)(2,1)}), bf16[8,8,1536]{2,1,0:T(8,128)(2,1)S(1)}, u32[]{:S(2)}, u32[]{:S(2)}) %all-to-all-start.5) | async-done | bytes 196640 | tf_op jit(solution)/shard_map/all_to_all | solution.py:33
  163.2 0.6 reduce_sum.35
  (20 shorter events, 0.3 us)
Async XLA Ops:
  0.6 105.9 %copy-start = (bf16[1536,384]{1,0:T(8,128)(2,1)S(1)}, bf16[1536,384]{1,0:T(8,128)(2,1)}, u32[]{:S(2)}) copy-start(bf16[1536,384]{1,0:T(8,128)(2,1)} %param.8) | copy-start | bytes 3538948
  26.5 23.5 %copy-start.7 = (bf16[384,1536]{1,0:T(8,128)(2,1)S(1)}, bf16[384,1536]{1,0:T(8,128)(2,1)}, u32[]{:S(2)}) copy-start(bf16[384,1536]{1,0:T(8,128)(2,1)} %param.9) | copy-start | bytes 3538948
  50.0 1.1 copy-start.1
  51.1 21.2 %copy-start.6 = (bf16[64,384]{1,0:T(8,128)(2,1)S(1)}, bf16[64,384]{1,0:T(8,128)(2,1)}, u32[]{:S(2)}) copy-start(bf16[64,384]{1,0:T(8,128)(2,1)} %param.7) | copy-start | bytes 147460
  100.1 23.0 %all-to-all-start.6 = ((bf16[8,8,8,1536]{3,2,1,0:T(8,128)(2,1)}), bf16[8,8,8,1536]{3,2,1,0:T(8,128)(2,1)S(1)}, u32[]{:S(2)}, u32[]{:S(2)}) async-start(bf16[8,8,8,1536]{3,2,1,0:T(8,128)(2,1)} %broadcast_in_dim.31), calls=%async_computation.6 | async-start | bytes 3145728 | tf_op jit(solution)/shard_map/all_to_all | solution.py:33
  105.8 0.7 copy-start.3
  123.1 1.2 copy-start.2
  123.1 6.7 %copy-start.4 = (bf16[8,8,8,384]{3,2,1,0:T(8,128)(2,1)S(1)}, bf16[8,8,8,384]{3,2,1,0:T(8,128)(2,1)}, u32[]{:S(2)}) copy-start(bf16[8,8,8,384]{3,2,1,0:T(8,128)(2,1)} %copy-done.3) | copy-start | bytes 1179652
  124.3 23.9 %all-to-all-start.4 = ((bf16[8,64,1536]{2,1,0:T(8,128)(2,1)}), bf16[8,64,1536]{2,1,0:T(8,128)(2,1)S(1)}, u32[]{:S(2)}, u32[]{:S(2)}) async-start(bf16[8,64,1536]{2,1,0:T(8,128)(2,1)} %bitcast.12), calls=%async_computation.4 | async-start | bytes 3145728 | tf_op jit(solution)/shard_map/all_to_all | solution.py:33
  133.3 19.2 %copy-start.5 = (bf16[8,8,8,384]{3,2,1,0:T(8,128)(2,1)S(1)}, bf16[8,8,8,384]{3,2,1,0:T(8,128)(2,1)}, u32[]{:S(2)}) copy-start(bf16[8,8,8,384]{3,2,1,0:T(8,128)(2,1)} %get-tuple-element.3) | copy-start | bytes 1179652
  149.1 14.1 %all-to-all-start.5 = ((bf16[8,8,1536]{2,1,0:T(8,128)(2,1)}), bf16[8,8,1536]{2,1,0:T(8,128)(2,1)S(1)}, u32[]{:S(2)}, u32[]{:S(2)}) async-start(bf16[8,8,1536]{2,1,0:T(8,128)(2,1)} %bitcast.13), calls=%async_computation.5 | async-start | bytes 393216 | tf_op jit(solution)/shard_map/all_to_all | solution.py:33

commit v2 on v1

--- a/solution.py
+++ b/solution.py
@@ -37,6 +37,16 @@
     return swap(jnp.broadcast_to(block[None], (size,) + block.shape), axis)
 
 
+def add_up(blocks):
+    parts = [blocks[i].astype(jnp.float32) for i in range(blocks.shape[0])]
+    while len(parts) > 1:
+        parts = [
+            parts[i] + parts[i + 1] if i + 1 < len(parts) else parts[i]
+            for i in range(0, len(parts), 2)
+        ]
+    return parts[0]
+
+
 def make(sizes):
     nx, ny, nz = sizes
 
@@ -44,35 +54,43 @@
         tokens, width = inputs.shape
         rows_z, hidden_width = preact.shape
         total = nx * ny * tokens
-        both = gather(jnp.stack([inputs, out_grad]), "gx", nx)
-        rows_dy = gather(both[:, 1], "gy", ny).reshape(total, width)
-        rows_x = gather(both[:, 0], "gy", ny).reshape(total, width)
+        span = nx * tokens
+        near_dy = gather(out_grad, "gx", nx).reshape(span, width)
+        both = gather(jnp.concatenate([near_dy, inputs]), "gy", ny)
+        rows_dy = both[:, :span].reshape(total, width)
+        near_x = both[:, span:].reshape(ny * tokens, width)
+        rows_x = lax.all_gather(near_x, "gx", axis=0, tiled=True)
+
+        def turn(block, outer, inner):
+            block = block.reshape(outer, inner, tokens, -1)
+            return block.transpose(1, 0, 2, 3).reshape(total, -1)
 
         partial = contract_rows(rows_dy, w_out).astype(jnp.bfloat16)
-        partial = partial.reshape(ny, nx, tokens, hidden_width).transpose(1, 0, 2, 3)
-        partial = swap(partial.reshape(nz, rows_z, hidden_width), "gz")
-        grad_hidden = jnp.sum(partial.astype(jnp.float32), axis=0)
+        partial = turn(partial, ny, nx)
+        grad_hidden = add_up(swap(partial.reshape(nz, rows_z, hidden_width), "gz"))
 
         value_local, slope_local = gelu_parts(preact.astype(jnp.float32))
         grad_pre = (grad_hidden * slope_local).astype(jnp.bfloat16)
         hidden_local = value_local.astype(jnp.bfloat16)
-        pair = gather(jnp.stack([grad_pre, hidden_local]), "gz", nz)
+        pair = lax.all_gather(
+            jnp.concatenate([grad_pre, hidden_local], axis=1), "gz", axis=0, tiled=True
+        )
+        grad_all, hidden_all = pair[:, :hidden_width], pair[:, hidden_width:]
 
-        def by_gy(block):
-            block = block.reshape(nx, ny, tokens, hidden_width)
-            return block.transpose(1, 0, 2, 3).reshape(total, hidden_width)
+        part_in = contract_rows(turn(grad_all, nx, ny), w_in).astype(jnp.bfloat16)
+        part_in = swap(part_in.reshape(ny, span, width), "gy")
+        grad_w_in = contract_cols(rows_x, grad_all).astype(jnp.bfloat16)
+        part_in, grad_w_in = lax.optimization_barrier((part_in, grad_w_in))
+        part_in = add_up(part_in)
+        part_in = part_in.astype(jnp.bfloat16).reshape(nx, tokens, width)
+        grad_input = add_up(swap(part_in, "gx")).astype(jnp.bfloat16)
 
-        grad_all, hidden_all = by_gy(pair[:, 0]), by_gy(pair[:, 1])
-
-        part_in = contract_rows(grad_all, w_in).astype(jnp.bfloat16)
-        part_in = swap(part_in.reshape(ny, nx * tokens, width), "gy")
-        part_in = jnp.sum(part_in.astype(jnp.float32), axis=0).astype(jnp.bfloat16)
-        part_in = swap(part_in.reshape(nx, tokens, width), "gx")
-        grad_input = jnp.sum(part_in.astype(jnp.float32), axis=0).astype(jnp.bfloat16)
-
-        grad_w_out = contract_cols(hidden_all, rows_dy).astype(jnp.bfloat16)
-        grad_w_in = contract_cols(rows_x, grad_all).astype(jnp.bfloat16)
-        return (grad_input, grad_w_in, grad_w_out)
+        grad_w_out = contract_cols(turn(hidden_all, nx, ny), rows_dy)
+        return (
+            grad_input,
+            grad_w_in,
+            grad_w_out.astype(jnp.bfloat16),
+        )
 
     return on_device
 

time: 164 us -> 148 us (0.902)
  the two profiles are of different devices: /device:TPU:10 before, /device:TPU:8 now
where the time goes in v2:
time: 148 us; the launch traced here: 147 us
  blocking collectives  62.9 us (42%)
  waiting for transfers between devices  39.3 us (27%)
  between operations  14.1 us (10%)
  starting transfers between devices  13.4 us (9%)
  matrix products  9.82 us (7%)
  local copies, waits for them, and re-layouts  5.15 us (3%)
  other arithmetic  2.4 us (2%)
    all_to_all x2, blocking collectives, swap(): return lax.all_to_all(blocks, axis, split_axis=0, concat_axis=0, tiled=True)  46.5 us
    all_to_all x3, waiting for transfers between devices, swap(): return lax.all_to_all(blocks, axis, split_axis=0, concat_axis=0, tiled=True)  34.5 us
    all_gather x1, blocking collectives, on_device(): lax.all_gather(jnp.concatenate([grad_pre, hidden_local], axis=1), 'gz', a...  16.4 us
    all_to_all x3, starting transfers between devices, swap(): return lax.all_to_all(blocks, axis, split_axis=0, concat_axis=0, tiled=True)  13.4 us
    dot_general x2, matrix products, contract_cols(): lax.dot_general(left, right, (((0,), (0,)), ((), ())), preferred_element_...  6.66 us
    all_gather x1, waiting for transfers between devices, on_device(): rows_x = lax.all_gather(near_x, 'gx', axis=0, tiled=True)  4.77 us
    dot_general x2, matrix products, contract_rows(): lax.dot_general(left, right, (((1,), (1,)), ((), ())), preferred_element_...  3.16 us
  transfers between devices with their start and end apart: 4, of which 4 were waited for; matrix products, arithmetic and copies ran while one was open for 7% of the time, Pallas kernels for 0%

profile of v2, /device:TPU:8, one launch (start us, length us, event | category | flops | bytes accessed | tf_op | source)
XLA Modules:
  0.0 147.1 jit_solution(1992764161042813060)
XLA Ops:
  7.2 0.8 broadcast_in_dim.4
  8.0 20.6 %all_to_all.25 = bf16[8,8,1536]{2,1,0:T(8,128)(2,1)S(1)} all-to-all(bf16[8,8,1536]{2,1,0:T(8,128)(2,1)S(1)} %broadcast_in_dim.4), channel_id=1, replica_groups=mesh['gx'=8,'gy'=8,'gz'=8] {'gx'}, dimensions={0} | all-to-all | bytes 393216 | tf_op jit(solution)/shard_map/all_to_all | solution.py:33
  28.6 0.8 pad_maximum_fusion
  29.5 25.9 %all_to_all.26 = bf16[8,72,1536]{2,1,0:T(8,128)(2,1)S(1)} all-to-all(bf16[8,72,1536]{2,1,0:T(8,128)(2,1)S(1)} %broadcast_in_dim.5), channel_id=1, replica_groups=mesh['gx'=8,'gy'=8,'gz'=8] {'gy'}, dimensions={0} | all-to-all | bytes 3538944 | tf_op jit(solution)/shard_map/all_to_all | solution.py:33
  55.4 0.1 slice.112
  55.5 1.7 %copy-done.4 = bf16[384,1536]{1,0:T(8,128)(2,1)S(1)} copy-done((bf16[384,1536]{1,0:T(8,128)(2,1)S(1)}, bf16[384,1536]{1,0:T(8,128)(2,1)}, u32[]{:S(2)}) %copy-start.4) | copy-done | bytes 1179672
  57.2 1.0 convolution_convert_fusion.3
  58.2 0.8 copy.14
  59.0 6.2 %all-to-all-start.2 = ((bf16[8,64,384]{2,1,0:T(8,128)(2,1)}), bf16[8,64,384]{2,1,0:T(8,128)(2,1)S(1)}, u32[]{:S(2)}, u32[]{:S(2)}) async-start(bf16[8,64,384]{2,1,0:T(8,128)(2,1)} %bitcast.35), calls=%async_computation.2 | async-start | bytes 786432 | tf_op jit(solution)/shard_map/all_to_all | solution.py:33
  65.2 0.7 slice_bitcast_fusion
  65.9 14.6 %all-to-all-done.2 = bf16[8,64,384]{2,1,0:T(8,128)(2,1)S(1)} async-done(((bf16[8,64,384]{2,1,0:T(8,128)(2,1)}), bf16[8,64,384]{2,1,0:T(8,128)(2,1)S(1)}, u32[]{:S(2)}, u32[]{:S(2)}) %all-to-all-start.2) | async-done | bytes 393248 | tf_op jit(solution)/shard_map/all_to_all | solution.py:33
  80.6 0.1 fusion.7
  80.7 16.4 %all_gather.6 = bf16[512,768]{1,0:T(8,128)(2,1)S(1)} all-gather(bf16[64,768]{1,0:T(8,128)(2,1)S(1)} %pad_maximum_fusion.1), channel_id=1, replica_groups=mesh['gx'=8,'gy'=8,'gz'=8] {'gz'}, dimensions={0}, use_global_device_ids=true | all-gather | bytes 884736 | tf_op jit(solution)/shard_map/all_gather | solution.py:75
  97.2 0.8 fusion.14
  98.0 2.2 %convolution_convert_fusion = bf16[512,1536]{1,0:T(8,128)(2,1)} fusion(bf16[512,384]{1,0:T(8,128)(2,1)S(1)} %bitcast.36, bf16[1536,384]{1,0:T(8,128)(2,1)S(1)} %copy-done), kind=kOutput, calls=%fused_computation | convolution fusion | flops 604766208 | bytes 3145728 | tf_op jit(solution)/shard_map/dot_general | solution.py:21
  100.2 3.8 %all-to-all-start.3 = ((bf16[8,64,1536]{2,1,0:T(8,128)(2,1)}), bf16[8,64,1536]{2,1,0:T(8,128)(2,1)S(1)}, u32[]{:S(2)}, u32[]{:S(2)}) async-start(bf16[8,64,1536]{2,1,0:T(8,128)(2,1)} %bitcast.32), calls=%async_computation.3 | async-start | bytes 3145728 | tf_op jit(solution)/shard_map/all_to_all | solution.py:33
  104.0 4.8 %all-gather.2.cloned.1.call-done = bf16[512,1536]{1,0:T(8,128)(2,1)} async-done(((bf16[64,1536]{1,0:T(8,128)(2,1)}), bf16[512,1536]{1,0:T(8,128)(2,1)}) %all-gather.2.cloned.1.call-update) | async-done | bytes 1572880 | tf_op jit(solution)/shard_map/all_gather | solution.py:62
  108.8 3.4 %convolution_convert_fusion.2 = bf16[1536,384]{1,0:T(8,128)(2,1)} fusion(bf16[512,1536]{1,0:T(8,128)(2,1)} %all-gather.2.cloned.1.call-done, bf16[512,768]{1,0:T(8,128)(2,1)S(1)} %all_gather.6), kind=kOutput, calls=%fused_computation.2 | convolution fusion | flops 604569600 | bytes 3145728 | tf_op jit(solution)/shard_map/dot_general | solution.py:27
  112.2 12.8 %all-to-all-done.3 = bf16[8,64,1536]{2,1,0:T(8,128)(2,1)S(1)} async-done(((bf16[8,64,1536]{2,1,0:T(8,128)(2,1)}), bf16[8,64,1536]{2,1,0:T(8,128)(2,1)S(1)}, u32[]{:S(2)}, u32[]{:S(2)}) %all-to-all-start.3) | async-done | bytes 1572896 | tf_op jit(solution)/shard_map/all_to_all | solution.py:33
  125.0 0.9 fusion
  125.8 3.4 %all-to-all-start.4 = ((bf16[8,8,1536]{2,1,0:T(8,128)(2,1)}), bf16[8,8,1536]{2,1,0:T(8,128)(2,1)S(1)}, u32[]{:S(2)}, u32[]{:S(2)}) async-start(bf16[8,8,1536]{2,1,0:T(8,128)(2,1)} %fusion), calls=%async_computation.4 | async-start | bytes 393216 | tf_op jit(solution)/shard_map/all_to_all | solution.py:33
  129.3 3.2 %convolution_convert_fusion.1 = bf16[384,1536]{1,0:T(8,128)(2,1)} fusion(bf16[512,384]{1,0:T(8,128)(2,1)S(1)} %bitcast.40, bf16[512,1536]{1,0:T(8,128)(2,1)} %bitcast.34), kind=kOutput, calls=%fused_computation.1 | convolution fusion | flops 604569600 | bytes 3145728 | tf_op jit(solution)/shard_map/dot_general | solution.py:27
  132.5 7.1 %all-to-all-done.4 = bf16[8,8,1536]{2,1,0:T(8,128)(2,1)S(1)} async-done(((bf16[8,8,1536]{2,1,0:T(8,128)(2,1)}), bf16[8,8,1536]{2,1,0:T(8,128)(2,1)S(1)}, u32[]{:S(2)}, u32[]{:S(2)}) %all-to-all-start.4) | async-done | bytes 196640 | tf_op jit(solution)/shard_map/all_to_all | solution.py:33
  139.6 0.6 fusion.12
  (15 shorter events, 0.3 us)
Async XLA Ops:
  7.2 90.9 %copy-start = (bf16[1536,384]{1,0:T(8,128)(2,1)S(1)}, bf16[1536,384]{1,0:T(8,128)(2,1)}, u32[]{:S(2)}) copy-start(bf16[1536,384]{1,0:T(8,128)(2,1)} %param.8) | copy-start | bytes 3538948
  55.4 1.8 %copy-start.4 = (bf16[384,1536]{1,0:T(8,128)(2,1)S(1)}, bf16[384,1536]{1,0:T(8,128)(2,1)}, u32[]{:S(2)}) copy-start(bf16[384,1536]{1,0:T(8,128)(2,1)} %param.9) | copy-start | bytes 3538948
  55.5 2.7 %copy-start.1 = (bf16[8,64,1536]{2,1,0:T(8,128)(2,1)}, bf16[8,64,1536]{2,1,0:T(8,128)(2,1)S(1)}, u32[]{:S(2)}) copy-start(bf16[8,64,1536]{2,1,0:T(8,128)(2,1)S(1)} %slice.112) | copy-start | bytes 4718596
  58.2 22.4 %copy-start.3 = (bf16[64,384]{1,0:T(8,128)(2,1)S(1)}, bf16[64,384]{1,0:T(8,128)(2,1)}, u32[]{:S(2)}) copy-start(bf16[64,384]{1,0:T(8,128)(2,1)} %param.7) | copy-start | bytes 147460
  59.0 21.6 %all-to-all-start.2 = ((bf16[8,64,384]{2,1,0:T(8,128)(2,1)}), bf16[8,64,384]{2,1,0:T(8,128)(2,1)S(1)}, u32[]{:S(2)}, u32[]{:S(2)}) async-start(bf16[8,64,384]{2,1,0:T(8,128)(2,1)} %bitcast.35), calls=%async_computation.2 | async-start | bytes 786432 | tf_op jit(solution)/shard_map/all_to_all | solution.py:33
  65.2 43.6 %all-gather.2.cloned.1.call-start = ((), (), s32[]{:S(2)}) async-start(), calls=%async_computation.5 | async-start | bytes 1769472 | tf_op jit(solution)/shard_map/all_gather | solution.py:62
  100.2 24.8 %all-to-all-start.3 = ((bf16[8,64,1536]{2,1,0:T(8,128)(2,1)}), bf16[8,64,1536]{2,1,0:T(8,128)(2,1)S(1)}, u32[]{:S(2)}, u32[]{:S(2)}) async-start(bf16[8,64,1536]{2,1,0:T(8,128)(2,1)} %bitcast.32), calls=%async_computation.3 | async-start | bytes 3145728 | tf_op jit(solution)/shard_map/all_to_all | solution.py:33
  112.2 17.0 %copy-start.2 = (bf16[512,384]{1,0:T(8,128)(2,1)S(1)}, bf16[512,384]{1,0:T(8,128)(2,1)}, u32[]{:S(2)}) copy-start(bf16[512,384]{1,0:T(8,128)(2,1)} %get-tuple-element.7) | copy-start | bytes 1179652
  125.8 13.8 %all-to-all-start.4 = ((bf16[8,8,1536]{2,1,0:T(8,128)(2,1)}), bf16[8,8,1536]{2,1,0:T(8,128)(2,1)S(1)}, u32[]{:S(2)}, u32[]{:S(2)}) async-start(bf16[8,8,1536]{2,1,0:T(8,128)(2,1)} %fusion), calls=%async_computation.4 | async-start | bytes 393216 | tf_op jit(solution)/shard_map/all_to_all | solution.py:33
Sparse Core Ops, SparseCore 0:
  68.7 40.0 all-gather.1

commit v3 on v2

v3 whole, which is shorter than its diff:
```python
import jax
import jax.numpy as jnp
from jax import lax
from jax.sharding import Mesh
from jax.sharding import PartitionSpec as P

gelu_scale = 0.7978845608028654
cubic_coef = 0.044715


def gelu_parts(pre_float):
    tanh_arg = gelu_scale * (pre_float + cubic_coef * pre_float * pre_float * pre_float)
    tangent = jnp.tanh(tanh_arg)
    value = 0.5 * pre_float * (1.0 + tangent)
    slope = 0.5 * (1.0 + tangent) + 0.5 * pre_float * (1.0 - tangent * tangent) * gelu_scale * (
        1.0 + 3.0 * cubic_coef * pre_float * pre_float
    )
    return (value, slope)


def contract_rows(left, right):
    return lax.dot_general(
        left, right, (((1,), (1,)), ((), ())), preferred_element_type=jnp.float32
    )


def contract_cols(left, right):
    return lax.dot_general(
        left, right, (((0,), (0,)), ((), ())), preferred_element_type=jnp.float32
    )


def swap(blocks, axis):
    return lax.all_to_all(blocks, axis, split_axis=0, concat_axis=0, tiled=True)


def gather(block, axis, size):
    return swap(jnp.broadcast_to(block[None], (size,) + block.shape), axis)


def add_up(blocks):
    parts = [blocks[i].astype(jnp.float32) for i in range(blocks.shape[0])]
    while len(parts) > 1:
        parts = [
            parts[i] + parts[i + 1] if i + 1 < len(parts) else parts[i]
            for i in range(0, len(parts), 2)
        ]
    return parts[0]


def make(sizes):
    nx, ny, nh, nc = sizes

    def on_device(inputs, out_grad, preact, w_in, w_out):
        tokens, width = inputs.shape
        rows_z, hidden_width = preact.shape
        total = nx * ny * tokens
        span = nx * tokens
        out_grad, first = lax.optimization_barrier((out_grad, lax.axis_index("gc") == 0))
        near_dy = gather(out_grad, "gx", nx).reshape(span, width)
        both = gather(jnp.concatenate([near_dy, inputs]), "gy", ny)
        rows_dy = both[:, :span].reshape(total, width)
        near_x = both[:, span:].reshape(ny * tokens, width)
        rows_x = lax.all_gather(near_x, "gx", axis=0, tiled=True)

        partial = contract_rows(rows_dy, w_out)
        partial = partial.reshape(ny, nh, nc, tokens, hidden_width)
        partial = partial.transpose(2, 1, 0, 3, 4).reshape(nc, nh * rows_z, hidden_width)
        theirs = jnp.where(first, partial[1], partial[0])
        mine = jnp.where(first, partial[0], partial[1])
        theirs = lax.all_gather(theirs, "gc", axis=0)
        mine = mine + jnp.where(first, theirs[1], theirs[0])
        chips = lax.all_gather(
            jnp.concatenate([mine.astype(jnp.bfloat16), preact]), "gh", axis=0
        )
        grad_hidden = add_up(chips[:, : nh * rows_z])
        pre = chips[:, nh * rows_z :].reshape(nh * rows_z, hidden_width)

        value, slope = gelu_parts(pre.astype(jnp.float32))
        grad_pre = (grad_hidden * slope).astype(jnp.bfloat16)
        pair = lax.all_gather(
            jnp.concatenate([grad_pre, value.astype(jnp.bfloat16)], axis=1), "gc", axis=0
        )
        pair = pair.reshape(nc, nh, ny, tokens, 2 * hidden_width)

        def by_gx(block):
            return block.transpose(1, 0, 2, 3, 4).reshape(total, hidden_width)

        def by_gy(block):
            return block.transpose(2, 1, 0, 3, 4).reshape(total, hidden_width)

        grad_all, hidden_all = pair[..., :hidden_width], pair[..., hidden_width:]

        part_in = contract_rows(by_gy(grad_all), w_in).astype(jnp.bfloat16)
        part_in = swap(part_in.reshape(ny, span, width), "gy")
        grad_w_in = contract_cols(rows_x, by_gx(grad_all)).astype(jnp.bfloat16)
        grad_w_out = contract_cols(by_gy(hidden_all), rows_dy).astype(jnp.bfloat16)
        part_in, grad_w_in, grad_w_out = lax.optimization_barrier(
            (part_in, grad_w_in, grad_w_out)
        )
        part_in = add_up(part_in)
        part_in = part_in.astype(jnp.bfloat16).reshape(nx, tokens, width)
        grad_input = add_up(swap(part_in, "gx")).astype(jnp.bfloat16)
        return (grad_input, grad_w_in, grad_w_out)

    return on_device


def solution(mesh):
    nx, ny, nz = (mesh.shape[a] for a in ("gx", "gy", "gz"))
    nc = 2
    sizes = (nx, ny, nz // nc, nc)
    mesh = Mesh(mesh.devices.reshape(sizes), ("gx", "gy", "gh", "gc"))
    tokens, features = ("gx", "gy"), ("gh", "gc")
    in_specs = (
        P(tokens, features),
        P(tokens, features),
        P(features, tokens),
        P(features, tokens),
        P(tokens, features),
    )
    out_specs = (P(tokens, features), P(features, tokens), P(tokens, features))
    return jax.shard_map(
        make(sizes), mesh=mesh, in_specs=in_specs, out_specs=out_specs, check_vma=False
    )
```

time: 148 us -> 137 us (0.926)
  waiting for transfers between devices: 39.3 us -> 14.1 us
  blocking collectives: 62.9 us -> 87.2 us
  starting transfers between devices: 13.4 us -> 5.43 us
    all_to_all x3 -> x1, waiting for transfers between devices: 34.5 us -> 14.1 us  [swap(): return lax.all_to_all(blocks, axis, split_axis=0, concat_axis=0, tiled=True)]
    all_to_all x2 -> x3, blocking collectives: 46.5 us -> 59.6 us  [swap(): return lax.all_to_all(blocks, axis, split_axis=0, concat_axis=0, tiled=True)]
    all_gather x1 -> x3, blocking collectives: 16.4 us -> 27.6 us  [the longest x1 22.9 us: on_device(): lax.all_gather(jnp.concatenate([mine.astype(jnp.bfloat16), preact]), 'gh'...]
    all_to_all x3 -> x1, starting transfers between devices: 13.4 us -> 5.39 us  [swap(): return lax.all_to_all(blocks, axis, split_axis=0, concat_axis=0, tiled=True)]
    all_gather x1, waiting for transfers between devices: 4.77 us -> 0.01 us  [on_device(): rows_x = lax.all_gather(near_x, 'gx', axis=0, tiled=True)]
  transfers between devices with their start and end apart: 4 -> 2, of which waited for: 4 -> 1; matrix products, arithmetic and copies ran while one was open for 7% -> 7% of each run, Pallas kernels for 0% -> 0%
where the time goes in v3:
time: 137 us
  blocking collectives  87.2 us (64%)
  between operations  14.2 us (10%)
  waiting for transfers between devices  14.1 us (10%)
  matrix products  8.41 us (6%)
  starting transfers between devices  5.43 us (4%)
  local copies, waits for them, and re-layouts  5.09 us (4%)
  other arithmetic  2.19 us (2%)
    all_to_all x3, blocking collectives, swap(): return lax.all_to_all(blocks, axis, split_axis=0, concat_axis=0, tiled=True)  59.6 us
    all_gather x1, blocking collectives, on_device(): lax.all_gather(jnp.concatenate([mine.astype(jnp.bfloat16), preact]), 'gh'...  22.9 us
    all_to_all x1, waiting for transfers between devices, swap(): return lax.all_to_all(blocks, axis, split_axis=0, concat_axis=0, tiled=True)  14.1 us
    all_to_all x1, starting transfers between devices, swap(): return lax.all_to_all(blocks, axis, split_axis=0, concat_axis=0, tiled=True)  5.39 us
    dot_general x2, matrix products, contract_cols(): lax.dot_general(left, right, (((0,), (0,)), ((), ())), preferred_element_...  5.25 us
    dot_general x2, matrix products, contract_rows(): lax.dot_general(left, right, (((1,), (1,)), ((), ())), preferred_element_...  3.16 us
    unnamed x10, local copies, waits for them, and re-layouts  2.95 us
  transfers between devices with their start and end apart: 2, of which 1 were waited for; matrix products, arithmetic and copies ran while one was open for 7% of the time, Pallas kernels for 0%

profile of v3, /device:TPU:8, one launch (start us, length us, event | category | flops | bytes accessed | tf_op | source)
XLA Modules:
  0.0 136.7 jit_solution(6669645997315626229)
XLA Ops:
  7.2 0.8 broadcast_in_dim.4
  8.1 20.6 %all_to_all.20 = bf16[8,8,1536]{2,1,0:T(8,128)(2,1)S(1)} all-to-all(bf16[8,8,1536]{2,1,0:T(8,128)(2,1)S(1)} %broadcast_in_dim.4), channel_id=1, replica_groups=mesh['gx'=8,'gy'=8,'gh'=4,'gc'=2] {'gx'}, dimensions={0} | all-to-all | bytes 393216 | tf_op jit(solution)/shard_map/all_to_all | solution.py:34
  28.7 0.8 pad_maximum_fusion.2
  29.4 0.1 broadcast_in_dim.5
  29.5 25.9 %all_to_all.21 = bf16[8,72,1536]{2,1,0:T(8,128)(2,1)S(1)} all-to-all(bf16[8,72,1536]{2,1,0:T(8,128)(2,1)S(1)} %broadcast_in_dim.5), channel_id=1, replica_groups=mesh['gx'=8,'gy'=8,'gh'=4,'gc'=2] {'gy'}, dimensions={0} | all-to-all | bytes 3538944 | tf_op jit(solution)/shard_map/all_to_all | solution.py:34
  55.4 0.7 slice_bitcast_fusion.3
  56.1 0.1 slice.125
  56.3 1.6 %copy-done.4 = bf16[384,1536]{1,0:T(8,128)(2,1)S(1)} copy-done((bf16[384,1536]{1,0:T(8,128)(2,1)S(1)}, bf16[384,1536]{1,0:T(8,128)(2,1)}, u32[]{:S(2)}) %copy-start.4) | copy-done | bytes 1179672
  57.9 1.0 convolution_bitcast_fusion
  58.9 0.1 slice_select_fusion.2
  59.1 2.4 %all_gather.19 = f32[2,256,384]{2,1,0:T(8,128)S(1)} all-gather(f32[1,256,384]{2,1,0:T(8,128)S(1)} %bitcast.57), channel_id=1, replica_groups=mesh['gx'=8,'gy'=8,'gh'=4,'gc'=2] {'gc'}, dimensions={0}, use_global_device_ids=true | all-gather | bytes 1179648 | tf_op jit(solution)/shard_map/all_gather | solution.py:71
  61.5 22.9 %all-gather = bf16[1280,384]{1,0:T(8,128)(2,1)S(1)} all-gather(bf16[320,384]{1,0:T(8,128)(2,1)S(1)} %pad_maximum_fusion.1), channel_id=2, replica_groups=mesh['gx'=8,'gy'=8,'gh'=4,'gc'=2] {'gh'}, dimensions={0}, use_global_device_ids=true | all-gather | bytes 1228800 | tf_op jit(solution)/shard_map/all_gather | solution.py:73
  84.5 0.4 fusion.7
  84.9 2.4 %all-gather.1 = bf16[512,768]{1,0:T(8,128)(2,1)S(1)} all-gather(bf16[256,768]{1,0:T(8,128)(2,1)S(1)} %pad_maximum_fusion), channel_id=3, replica_groups=mesh['gx'=8,'gy'=8,'gh'=4,'gc'=2] {'gc'}, dimensions={0}, use_global_device_ids=true | all-gather | bytes 1179648 | tf_op jit(solution)/shard_map/all_gather | solution.py:81
  87.3 0.2 slice_bitcast_fusion
  87.5 2.2 %convolution_convert_fusion = bf16[512,1536]{1,0:T(8,128)(2,1)} fusion(bf16[512,384]{1,0:T(8,128)(2,1)S(1)} %bitcast.56, bf16[1536,384]{1,0:T(8,128)(2,1)S(1)} %copy-done), kind=kOutput, calls=%fused_computation | convolution fusion | flops 604766208 | bytes 3145728 | tf_op jit(solution)/shard_map/dot_general | solution.py:22
  89.7 5.4 %all-to-all-start.2 = ((bf16[8,64,1536]{2,1,0:T(8,128)(2,1)}), bf16[8,64,1536]{2,1,0:T(8,128)(2,1)S(1)}, u32[]{:S(2)}, u32[]{:S(2)}) async-start(bf16[8,64,1536]{2,1,0:T(8,128)(2,1)} %bitcast.50), calls=%async_computation.2 | async-start | bytes 3145728 | tf_op jit(solution)/shard_map/all_to_all | solution.py:34
  95.2 1.3 copy-done.2
  96.5 1.8 %convolution_convert_fusion.1 = bf16[384,1536]{1,0:T(8,128)(2,1)} fusion(bf16[512,384]{1,0:T(8,128)(2,1)S(1)} %bitcast.60, bf16[512,1536]{1,0:T(8,128)(2,1)S(1)} %bitcast.55), kind=kOutput, calls=%fused_computation.1 | convolution fusion | flops 604569600 | bytes 3145728 | tf_op jit(solution)/shard_map/dot_general | solution.py:28
  98.3 3.4 %convolution_convert_fusion.2 = bf16[1536,384]{1,0:T(8,128)(2,1)} fusion(bf16[512,1536]{1,0:T(8,128)(2,1)} %all-gather.4.cloned.1.call-done, bf16[512,384]{1,0:T(8,128)(2,1)S(1)} %bitcast.59), kind=kOutput, calls=%fused_computation.2 | convolution fusion | flops 604569600 | bytes 3145728 | tf_op jit(solution)/shard_map/dot_general | solution.py:28
  101.7 14.1 %all-to-all-done.2 = bf16[8,64,1536]{2,1,0:T(8,128)(2,1)S(1)} async-done(((bf16[8,64,1536]{2,1,0:T(8,128)(2,1)}), bf16[8,64,1536]{2,1,0:T(8,128)(2,1)S(1)}, u32[]{:S(2)}, u32[]{:S(2)}) %all-to-all-start.2) | async-done | bytes 1572896 | tf_op jit(solution)/shard_map/all_to_all | solution.py:34
  115.8 0.2 fusion.15
  116.0 13.1 %all_to_all.22 = bf16[8,8,1536]{2,1,0:T(8,128)(2,1)S(1)} all-to-all(bf16[8,8,1536]{2,1,0:T(8,128)(2,1)S(1)} %fusion.15), channel_id=1, replica_groups=mesh['gx'=8,'gy'=8,'gh'=4,'gc'=2] {'gx'}, dimensions={0} | all-to-all | bytes 393216 | tf_op jit(solution)/shard_map/all_to_all | solution.py:34
  129.2 0.6 fusion.16
  (20 shorter events, 0.4 us)
Async XLA Ops:
  7.2 80.3 %copy-start = (bf16[1536,384]{1,0:T(8,128)(2,1)S(1)}, bf16[1536,384]{1,0:T(8,128)(2,1)}, u32[]{:S(2)}) copy-start(bf16[1536,384]{1,0:T(8,128)(2,1)} %param.8) | copy-start | bytes 3538948
  7.2 91.1 %all-gather.4.cloned.1.call-start = ((), (), s32[]{:S(2)}) async-start(), calls=%async_computation.4 | async-start | bytes 1769472 | tf_op jit(solution)/shard_map/all_gather | solution.py:64
  56.1 1.8 %copy-start.4 = (bf16[384,1536]{1,0:T(8,128)(2,1)S(1)}, bf16[384,1536]{1,0:T(8,128)(2,1)}, u32[]{:S(2)}) copy-start(bf16[384,1536]{1,0:T(8,128)(2,1)} %param.9) | copy-start | bytes 3538948
  56.3 2.6 %copy-start.1 = (bf16[8,64,1536]{2,1,0:T(8,128)(2,1)}, bf16[8,64,1536]{2,1,0:T(8,128)(2,1)S(1)}, u32[]{:S(2)}) copy-start(bf16[8,64,1536]{2,1,0:T(8,128)(2,1)S(1)} %slice.125) | copy-start | bytes 4718596
  59.0 2.5 %copy-start.3 = (bf16[64,384]{1,0:T(8,128)(2,1)S(1)}, bf16[64,384]{1,0:T(8,128)(2,1)}, u32[]{:S(2)}) copy-start(bf16[64,384]{1,0:T(8,128)(2,1)} %param.7) | copy-start | bytes 147460
  89.7 26.2 %all-to-all-start.2 = ((bf16[8,64,1536]{2,1,0:T(8,128)(2,1)}), bf16[8,64,1536]{2,1,0:T(8,128)(2,1)S(1)}, u32[]{:S(2)}, u32[]{:S(2)}) async-start(bf16[8,64,1536]{2,1,0:T(8,128)(2,1)} %bitcast.50), calls=%async_computation.2 | async-start | bytes 3145728 | tf_op jit(solution)/shard_map/all_to_all | solution.py:34
  95.1 1.4 %copy-start.2 = (bf16[8,64,1536]{2,1,0:T(8,128)(2,1)S(1)}, bf16[8,64,1536]{2,1,0:T(8,128)(2,1)}, u32[]{:S(2)}) copy-start(bf16[8,64,1536]{2,1,0:T(8,128)(2,1)} %copy-done.1) | copy-start | bytes 4718596
Sparse Core Ops, SparseCore 0:
  56.2 39.0 all-gather.3

commit v4 on v3

--- a/solution.py
+++ b/solution.py
@@ -56,9 +56,11 @@
         rows_z, hidden_width = preact.shape
         total = nx * ny * tokens
         span = nx * tokens
-        out_grad, first = lax.optimization_barrier((out_grad, lax.axis_index("gc") == 0))
-        near_dy = gather(out_grad, "gx", nx).reshape(span, width)
-        both = gather(jnp.concatenate([near_dy, inputs]), "gy", ny)
+        own, first = lax.optimization_barrier(
+            (jnp.stack([out_grad, inputs]), lax.axis_index("gc") == 0)
+        )
+        near_dy = gather(own[0], "gx", nx).reshape(span, width)
+        both = gather(jnp.concatenate([near_dy, own[1]]), "gy", ny)
         rows_dy = both[:, :span].reshape(total, width)
         near_x = both[:, span:].reshape(ny * tokens, width)
         rows_x = lax.all_gather(near_x, "gx", axis=0, tiled=True)

time: 137 us -> 136 us (level)
  no operation moved by 1% of the time
where the time goes in v4:
time: 136 us
  blocking collectives  87.2 us (64%)
  between operations  14.2 us (10%)
  waiting for transfers between devices  14.1 us (10%)
  matrix products  8.4 us (6%)
  starting transfers between devices  5.44 us (4%)
  local copies, waits for them, and re-layouts  4.27 us (3%)
  other arithmetic  2.3 us (2%)
    all_to_all x3, blocking collectives, swap(): return lax.all_to_all(blocks, axis, split_axis=0, concat_axis=0, tiled=True)  59.6 us
    all_gather x1, blocking collectives, on_device(): lax.all_gather(jnp.concatenate([mine.astype(jnp.bfloat16), preact]), 'gh'...  22.9 us
    all_to_all x1, waiting for transfers between devices, swap(): return lax.all_to_all(blocks, axis, split_axis=0, concat_axis=0, tiled=True)  14.1 us
    all_to_all x1, starting transfers between devices, swap(): return lax.all_to_all(blocks, axis, split_axis=0, concat_axis=0, tiled=True)  5.4 us
    dot_general x2, matrix products, contract_cols(): lax.dot_general(left, right, (((0,), (0,)), ((), ())), preferred_element_...  5.25 us
    dot_general x2, matrix products, contract_rows(): lax.dot_general(left, right, (((1,), (1,)), ((), ())), preferred_element_...  3.16 us
    unnamed x10, local copies, waits for them, and re-layouts  2.95 us
  transfers between devices with their start and end apart: 2, of which 1 were waited for; matrix products, arithmetic and copies ran while one was open for 7% of the time, Pallas kernels for 0%

profile of v4, /device:TPU:8, one launch (start us, length us, event | category | flops | bytes accessed | tf_op | source)
XLA Modules:
  0.0 135.9 jit_solution(8781361005516023449)
XLA Ops:
  7.2 0.8 pad_maximum_fusion.3
  8.1 20.6 %all_to_all.20 = bf16[8,8,1536]{2,1,0:T(8,128)(2,1)S(1)} all-to-all(bf16[8,8,1536]{2,1,0:T(8,128)(2,1)S(1)} %broadcast_in_dim.14), channel_id=1, replica_groups=mesh['gx'=8,'gy'=8,'gh'=4,'gc'=2] {'gx'}, dimensions={0} | all-to-all | bytes 393216 | tf_op jit(solution)/shard_map/all_to_all | solution.py:34
  28.7 0.1 broadcast_in_dim.15
  28.8 25.9 %all_to_all.21 = bf16[8,72,1536]{2,1,0:T(8,128)(2,1)S(1)} all-to-all(bf16[8,72,1536]{2,1,0:T(8,128)(2,1)S(1)} %broadcast_in_dim.15), channel_id=1, replica_groups=mesh['gx'=8,'gy'=8,'gh'=4,'gc'=2] {'gy'}, dimensions={0} | all-to-all | bytes 3538944 | tf_op jit(solution)/shard_map/all_to_all | solution.py:34
  54.7 0.7 slice_bitcast_fusion.3
  55.4 0.1 slice.133
  55.6 1.6 %copy-done.4 = bf16[384,1536]{1,0:T(8,128)(2,1)S(1)} copy-done((bf16[384,1536]{1,0:T(8,128)(2,1)S(1)}, bf16[384,1536]{1,0:T(8,128)(2,1)}, u32[]{:S(2)}) %copy-start.4) | copy-done | bytes 1179672
  57.2 1.0 convolution_bitcast_fusion
  58.2 0.1 slice_select_fusion.2
  58.4 2.4 %all_gather.19 = f32[2,256,384]{2,1,0:T(8,128)S(1)} all-gather(f32[1,256,384]{2,1,0:T(8,128)S(1)} %bitcast.63), channel_id=1, replica_groups=mesh['gx'=8,'gy'=8,'gh'=4,'gc'=2] {'gc'}, dimensions={0}, use_global_device_ids=true | all-gather | bytes 1179648 | tf_op jit(solution)/shard_map/all_gather | solution.py:73
  60.7 0.1 fusion.14
  60.8 22.9 %all-gather = bf16[1280,384]{1,0:T(8,128)(2,1)S(1)} all-gather(bf16[320,384]{1,0:T(8,128)(2,1)S(1)} %pad_maximum_fusion.1), channel_id=2, replica_groups=mesh['gx'=8,'gy'=8,'gh'=4,'gc'=2] {'gh'}, dimensions={0}, use_global_device_ids=true | all-gather | bytes 1228800 | tf_op jit(solution)/shard_map/all_gather | solution.py:75
  83.8 0.4 fusion.7
  84.2 2.4 %all-gather.1 = bf16[512,768]{1,0:T(8,128)(2,1)S(1)} all-gather(bf16[256,768]{1,0:T(8,128)(2,1)S(1)} %pad_maximum_fusion), channel_id=3, replica_groups=mesh['gx'=8,'gy'=8,'gh'=4,'gc'=2] {'gc'}, dimensions={0}, use_global_device_ids=true | all-gather | bytes 1179648 | tf_op jit(solution)/shard_map/all_gather | solution.py:83
  86.6 0.2 slice_bitcast_fusion
  86.8 2.2 %convolution_convert_fusion = bf16[512,1536]{1,0:T(8,128)(2,1)} fusion(bf16[512,384]{1,0:T(8,128)(2,1)S(1)} %bitcast.62, bf16[1536,384]{1,0:T(8,128)(2,1)S(1)} %copy-done), kind=kOutput, calls=%fused_computation | convolution fusion | flops 604766208 | bytes 3145728 | tf_op jit(solution)/shard_map/dot_general | solution.py:22
  89.0 5.4 %all-to-all-start.2 = ((bf16[8,64,1536]{2,1,0:T(8,128)(2,1)}), bf16[8,64,1536]{2,1,0:T(8,128)(2,1)S(1)}, u32[]{:S(2)}, u32[]{:S(2)}) async-start(bf16[8,64,1536]{2,1,0:T(8,128)(2,1)} %bitcast.56), calls=%async_computation.2 | async-start | bytes 3145728 | tf_op jit(solution)/shard_map/all_to_all | solution.py:34
  94.5 1.3 copy-done.2
  95.8 1.8 %convolution_convert_fusion.1 = bf16[384,1536]{1,0:T(8,128)(2,1)} fusion(bf16[512,384]{1,0:T(8,128)(2,1)S(1)} %bitcast.66, bf16[512,1536]{1,0:T(8,128)(2,1)S(1)} %bitcast.61), kind=kOutput, calls=%fused_computation.1 | convolution fusion | flops 604569600 | bytes 3145728 | tf_op jit(solution)/shard_map/dot_general | solution.py:28
  97.6 3.4 %convolution_convert_fusion.2 = bf16[1536,384]{1,0:T(8,128)(2,1)} fusion(bf16[512,1536]{1,0:T(8,128)(2,1)} %all-gather.4.cloned.1.call-done, bf16[512,384]{1,0:T(8,128)(2,1)S(1)} %bitcast.65), kind=kOutput, calls=%fused_computation.2 | convolution fusion | flops 604569600 | bytes 3145728 | tf_op jit(solution)/shard_map/dot_general | solution.py:28
  101.0 14.1 %all-to-all-done.2 = bf16[8,64,1536]{2,1,0:T(8,128)(2,1)S(1)} async-done(((bf16[8,64,1536]{2,1,0:T(8,128)(2,1)}), bf16[8,64,1536]{2,1,0:T(8,128)(2,1)S(1)}, u32[]{:S(2)}, u32[]{:S(2)}) %all-to-all-start.2) | async-done | bytes 1572896 | tf_op jit(solution)/shard_map/all_to_all | solution.py:34
  115.1 0.2 fusion.15
  115.3 13.1 %all_to_all.22 = bf16[8,8,1536]{2,1,0:T(8,128)(2,1)S(1)} all-to-all(bf16[8,8,1536]{2,1,0:T(8,128)(2,1)S(1)} %fusion.15), channel_id=1, replica_groups=mesh['gx'=8,'gy'=8,'gh'=4,'gc'=2] {'gx'}, dimensions={0} | all-to-all | bytes 393216 | tf_op jit(solution)/shard_map/all_to_all | solution.py:34
  128.5 0.6 fusion.16
  (22 shorter events, 0.4 us)
Async XLA Ops:
  7.2 79.6 %copy-start = (bf16[1536,384]{1,0:T(8,128)(2,1)S(1)}, bf16[1536,384]{1,0:T(8,128)(2,1)}, u32[]{:S(2)}) copy-start(bf16[1536,384]{1,0:T(8,128)(2,1)} %param.8) | copy-start | bytes 3538948
  7.2 90.4 %all-gather.4.cloned.1.call-start = ((), (), s32[]{:S(2)}) async-start(), calls=%async_computation.4 | async-start | bytes 1769472 | tf_op jit(solution)/shard_map/all_gather | solution.py:66
  55.4 1.8 %copy-start.4 = (bf16[384,1536]{1,0:T(8,128)(2,1)S(1)}, bf16[384,1536]{1,0:T(8,128)(2,1)}, u32[]{:S(2)}) copy-start(bf16[384,1536]{1,0:T(8,128)(2,1)} %param.9) | copy-start | bytes 3538948
  55.6 2.6 %copy-start.1 = (bf16[8,64,1536]{2,1,0:T(8,128)(2,1)}, bf16[8,64,1536]{2,1,0:T(8,128)(2,1)S(1)}, u32[]{:S(2)}) copy-start(bf16[8,64,1536]{2,1,0:T(8,128)(2,1)S(1)} %slice.133) | copy-start | bytes 4718596
  58.3 2.5 %copy-start.3 = (bf16[64,384]{1,0:T(8,128)(2,1)S(1)}, bf16[64,384]{1,0:T(8,128)(2,1)}, u32[]{:S(2)}) copy-start(bf16[64,384]{1,0:T(8,128)(2,1)} %param.7) | copy-start | bytes 147460
  89.0 26.2 %all-to-all-start.2 = ((bf16[8,64,1536]{2,1,0:T(8,128)(2,1)}), bf16[8,64,1536]{2,1,0:T(8,128)(2,1)S(1)}, u32[]{:S(2)}, u32[]{:S(2)}) async-start(bf16[8,64,1536]{2,1,0:T(8,128)(2,1)} %bitcast.56), calls=%async_computation.2 | async-start | bytes 3145728 | tf_op jit(solution)/shard_map/all_to_all | solution.py:34
  94.4 1.4 %copy-start.2 = (bf16[8,64,1536]{2,1,0:T(8,128)(2,1)S(1)}, bf16[8,64,1536]{2,1,0:T(8,128)(2,1)}, u32[]{:S(2)}) copy-start(bf16[8,64,1536]{2,1,0:T(8,128)(2,1)} %copy-done.1) | copy-start | bytes 4718596
Sparse Core Ops, SparseCore 0:
  55.5 39.0 all-gather.3

commit v5 on v4

--- a/solution.py
+++ b/solution.py
@@ -63,7 +63,7 @@
         both = gather(jnp.concatenate([near_dy, own[1]]), "gy", ny)
         rows_dy = both[:, :span].reshape(total, width)
         near_x = both[:, span:].reshape(ny * tokens, width)
-        rows_x = lax.all_gather(near_x, "gx", axis=0, tiled=True)
+        rows_x = gather(near_x, "gx", nx).reshape(total, width)
 
         partial = contract_rows(rows_dy, w_out)
         partial = partial.reshape(ny, nh, nc, tokens, hidden_width)

time: 136 us -> 131 us (0.963)
  between operations: 14.2 us -> 0.83 us
  starting transfers between devices: 5.44 us -> 9.46 us
  blocking collectives: 87.2 us -> 90 us
    all_to_all x1 -> x2, starting transfers between devices: 5.4 us -> 9.46 us  [swap(): return lax.all_to_all(blocks, axis, split_axis=0, concat_axis=0, tiled=True)]
    all_to_all x3, blocking collectives: 59.6 us -> 62.4 us  [swap(): return lax.all_to_all(blocks, axis, split_axis=0, concat_axis=0, tiled=True)]
    all_to_all x1 -> x2, waiting for transfers between devices: 14.1 us -> 15.1 us  [swap(): return lax.all_to_all(blocks, axis, split_axis=0, concat_axis=0, tiled=True)]
  transfers between devices with their start and end apart: 2 -> 2, of which waited for: 1 -> 2; matrix products, arithmetic and copies ran while one was open for 7% -> 7% of each run, Pallas kernels for 0% -> 0%
where the time goes in v5:
time: 131 us
  blocking collectives  90 us (69%)
  waiting for transfers between devices  15.1 us (12%)
  starting transfers between devices  9.46 us (7%)
  matrix products  8.4 us (6%)
  local copies, waits for them, and re-layouts  4.87 us (4%)
  other arithmetic  2.31 us (2%)
    all_to_all x3, blocking collectives, swap(): return lax.all_to_all(blocks, axis, split_axis=0, concat_axis=0, tiled=True)  62.4 us
    all_gather x1, blocking collectives, on_device(): lax.all_gather(jnp.concatenate([mine.astype(jnp.bfloat16), preact]), 'gh'...  22.8 us
    all_to_all x2, waiting for transfers between devices, swap(): return lax.all_to_all(blocks, axis, split_axis=0, concat_axis=0, tiled=True)  15.1 us
    all_to_all x2, starting transfers between devices, swap(): return lax.all_to_all(blocks, axis, split_axis=0, concat_axis=0, tiled=True)  9.46 us
    dot_general x2, matrix products, contract_cols(): lax.dot_general(left, right, (((0,), (0,)), ((), ())), preferred_element_...  5.24 us
    dot_general x2, matrix products, contract_rows(): lax.dot_general(left, right, (((1,), (1,)), ((), ())), preferred_element_...  3.16 us
    unnamed x10, local copies, waits for them, and re-layouts  2.95 us
  transfers between devices with their start and end apart: 2, of which 2 were waited for; matrix products, arithmetic and copies ran while one was open for 7% of the time, Pallas kernels for 0%

profile of v5, /device:TPU:8, one launch (start us, length us, event | category | flops | bytes accessed | tf_op | source)
XLA Modules:
  0.0 131.0 jit_solution(4231575063415225990)
XLA Ops:
  0.6 0.9 pad_maximum_fusion.3
  1.5 20.6 %all_to_all.25 = bf16[8,8,1536]{2,1,0:T(8,128)(2,1)S(1)} all-to-all(bf16[8,8,1536]{2,1,0:T(8,128)(2,1)S(1)} %broadcast_in_dim.21), channel_id=1, replica_groups=mesh['gx'=8,'gy'=8,'gh'=4,'gc'=2] {'gx'}, dimensions={0} | all-to-all | bytes 393216 | tf_op jit(solution)/shard_map/all_to_all | solution.py:34
  22.1 0.1 broadcast_in_dim.22
  22.3 25.9 %all_to_all.26 = bf16[8,72,1536]{2,1,0:T(8,128)(2,1)S(1)} all-to-all(bf16[8,72,1536]{2,1,0:T(8,128)(2,1)S(1)} %broadcast_in_dim.22), channel_id=1, replica_groups=mesh['gx'=8,'gy'=8,'gh'=4,'gc'=2] {'gy'}, dimensions={0} | all-to-all | bytes 3538944 | tf_op jit(solution)/shard_map/all_to_all | solution.py:34
  48.2 1.3 broadcast_in_dim.24
  49.4 4.3 %all-to-all-start.3 = ((bf16[8,64,1536]{2,1,0:T(8,128)(2,1)}), bf16[8,64,1536]{2,1,0:T(8,128)(2,1)}, u32[]{:S(2)}, u32[]{:S(2)}) async-start(bf16[8,64,1536]{2,1,0:T(8,128)(2,1)} %broadcast_in_dim.24), calls=%async_computation.3 | async-start | bytes 3145728 | tf_op jit(solution)/shard_map/all_to_all | solution.py:34
  53.7 0.1 slice.133
  53.9 1.6 %copy-done.4 = bf16[384,1536]{1,0:T(8,128)(2,1)S(1)} copy-done((bf16[384,1536]{1,0:T(8,128)(2,1)S(1)}, bf16[384,1536]{1,0:T(8,128)(2,1)}, u32[]{:S(2)}) %copy-start.4) | copy-done | bytes 1179672
  55.5 1.0 convolution_bitcast_fusion
  56.7 2.4 %all_gather.16 = f32[2,256,384]{2,1,0:T(8,128)S(1)} all-gather(f32[1,256,384]{2,1,0:T(8,128)S(1)} %bitcast.63), channel_id=1, replica_groups=mesh['gx'=8,'gy'=8,'gh'=4,'gc'=2] {'gc'}, dimensions={0}, use_global_device_ids=true | all-gather | bytes 1179648 | tf_op jit(solution)/shard_map/all_gather | solution.py:73
  59.2 22.8 %all-gather = bf16[1280,384]{1,0:T(8,128)(2,1)S(1)} all-gather(bf16[320,384]{1,0:T(8,128)(2,1)S(1)} %pad_maximum_fusion.1), channel_id=2, replica_groups=mesh['gx'=8,'gy'=8,'gh'=4,'gc'=2] {'gh'}, dimensions={0}, use_global_device_ids=true | all-gather | bytes 1228800 | tf_op jit(solution)/shard_map/all_gather | solution.py:75
  82.0 0.4 fusion.7
  82.5 2.4 %all-gather.1 = bf16[512,768]{1,0:T(8,128)(2,1)S(1)} all-gather(bf16[256,768]{1,0:T(8,128)(2,1)S(1)} %pad_maximum_fusion), channel_id=3, replica_groups=mesh['gx'=8,'gy'=8,'gh'=4,'gc'=2] {'gc'}, dimensions={0}, use_global_device_ids=true | all-gather | bytes 1179648 | tf_op jit(solution)/shard_map/all_gather | solution.py:83
  84.8 0.2 slice_bitcast_fusion
  85.1 2.2 %convolution_convert_fusion = bf16[512,1536]{1,0:T(8,128)(2,1)} fusion(bf16[512,384]{1,0:T(8,128)(2,1)S(1)} %bitcast.62, bf16[1536,384]{1,0:T(8,128)(2,1)S(1)} %copy-done), kind=kOutput, calls=%fused_computation | convolution fusion | flops 604766208 | bytes 3145728 | tf_op jit(solution)/shard_map/dot_general | solution.py:22
  87.2 3.5 %all-to-all-done.3 = bf16[8,64,1536]{2,1,0:T(8,128)(2,1)} async-done(((bf16[8,64,1536]{2,1,0:T(8,128)(2,1)}), bf16[8,64,1536]{2,1,0:T(8,128)(2,1)}, u32[]{:S(2)}, u32[]{:S(2)}) %all-to-all-start.3) | async-done | bytes 1572896 | tf_op jit(solution)/shard_map/all_to_all | solution.py:34
  90.7 5.2 %all-to-all-start.2 = ((bf16[8,64,1536]{2,1,0:T(8,128)(2,1)}), bf16[8,64,1536]{2,1,0:T(8,128)(2,1)S(1)}, u32[]{:S(2)}, u32[]{:S(2)}) async-start(bf16[8,64,1536]{2,1,0:T(8,128)(2,1)} %bitcast.19), calls=%async_computation.2 | async-start | bytes 3145728 | tf_op jit(solution)/shard_map/all_to_all | solution.py:34
  96.0 1.3 copy-done.2
  97.3 1.8 %convolution_convert_fusion.1 = bf16[384,1536]{1,0:T(8,128)(2,1)} fusion(bf16[512,384]{1,0:T(8,128)(2,1)S(1)} %bitcast.65, bf16[512,1536]{1,0:T(8,128)(2,1)S(1)} %bitcast.61), kind=kOutput, calls=%fused_computation.1 | convolution fusion | flops 604569600 | bytes 3145728 | tf_op jit(solution)/shard_map/dot_general | solution.py:28
  99.1 3.4 %convolution_convert_fusion.2 = bf16[1536,384]{1,0:T(8,128)(2,1)} fusion(bf16[512,1536]{1,0:T(8,128)(2,1)} %bitcast.21, bf16[512,384]{1,0:T(8,128)(2,1)S(1)} %bitcast.66), kind=kOutput, calls=%fused_computation.2 | convolution fusion | flops 604569600 | bytes 3145728 | tf_op jit(solution)/shard_map/dot_general | solution.py:28
  102.6 11.6 %all-to-all-done.2 = bf16[8,64,1536]{2,1,0:T(8,128)(2,1)S(1)} async-done(((bf16[8,64,1536]{2,1,0:T(8,128)(2,1)}), bf16[8,64,1536]{2,1,0:T(8,128)(2,1)S(1)}, u32[]{:S(2)}, u32[]{:S(2)}) %all-to-all-start.2) | async-done | bytes 1572896 | tf_op jit(solution)/shard_map/all_to_all | solution.py:34
  114.2 0.2 fusion.15
  114.4 16.0 %all_to_all.27 = bf16[8,8,1536]{2,1,0:T(8,128)(2,1)S(1)} all-to-all(bf16[8,8,1536]{2,1,0:T(8,128)(2,1)S(1)} %fusion.15), channel_id=1, replica_groups=mesh['gx'=8,'gy'=8,'gh'=4,'gc'=2] {'gx'}, dimensions={0} | all-to-all | bytes 393216 | tf_op jit(solution)/shard_map/all_to_all | solution.py:34
  130.3 0.6 fusion.16
  (22 shorter events, 0.5 us)
Async XLA Ops:
  0.6 84.4 %copy-start = (bf16[1536,384]{1,0:T(8,128)(2,1)S(1)}, bf16[1536,384]{1,0:T(8,128)(2,1)}, u32[]{:S(2)}) copy-start(bf16[1536,384]{1,0:T(8,128)(2,1)} %param.8) | copy-start | bytes 3538948
  49.4 41.3 %all-to-all-start.3 = ((bf16[8,64,1536]{2,1,0:T(8,128)(2,1)}), bf16[8,64,1536]{2,1,0:T(8,128)(2,1)}, u32[]{:S(2)}, u32[]{:S(2)}) async-start(bf16[8,64,1536]{2,1,0:T(8,128)(2,1)} %broadcast_in_dim.24), calls=%async_computation.3 | async-start | bytes 3145728 | tf_op jit(solution)/shard_map/all_to_all | solution.py:34
  53.7 1.8 %copy-start.4 = (bf16[384,1536]{1,0:T(8,128)(2,1)S(1)}, bf16[384,1536]{1,0:T(8,128)(2,1)}, u32[]{:S(2)}) copy-start(bf16[384,1536]{1,0:T(8,128)(2,1)} %param.9) | copy-start | bytes 3538948
  53.9 2.6 %copy-start.1 = (bf16[8,64,1536]{2,1,0:T(8,128)(2,1)}, bf16[8,64,1536]{2,1,0:T(8,128)(2,1)S(1)}, u32[]{:S(2)}) copy-start(bf16[8,64,1536]{2,1,0:T(8,128)(2,1)S(1)} %slice.133) | copy-start | bytes 4718596
  56.6 2.5 %copy-start.3 = (bf16[64,384]{1,0:T(8,128)(2,1)S(1)}, bf16[64,384]{1,0:T(8,128)(2,1)}, u32[]{:S(2)}) copy-start(bf16[64,384]{1,0:T(8,128)(2,1)} %param.7) | copy-start | bytes 147460
  90.7 23.4 %all-to-all-start.2 = ((bf16[8,64,1536]{2,1,0:T(8,128)(2,1)}), bf16[8,64,1536]{2,1,0:T(8,128)(2,1)S(1)}, u32[]{:S(2)}, u32[]{:S(2)}) async-start(bf16[8,64,1536]{2,1,0:T(8,128)(2,1)} %bitcast.19), calls=%async_computation.2 | async-start | bytes 3145728 | tf_op jit(solution)/shard_map/all_to_all | solution.py:34
  95.9 1.4 %copy-start.2 = (bf16[8,64,1536]{2,1,0:T(8,128)(2,1)S(1)}, bf16[8,64,1536]{2,1,0:T(8,128)(2,1)}, u32[]{:S(2)}) copy-start(bf16[8,64,1536]{2,1,0:T(8,128)(2,1)} %copy-done.1) | copy-start | bytes 4718596

commit v6 on v5

--- a/solution.py
+++ b/solution.py
@@ -61,7 +61,8 @@
         )
         near_dy = gather(own[0], "gx", nx).reshape(span, width)
         both = gather(jnp.concatenate([near_dy, own[1]]), "gy", ny)
-        rows_dy = both[:, :span].reshape(total, width)
+        rows_dy, both = lax.optimization_barrier((both[:, :span], both))
+        rows_dy = rows_dy.reshape(total, width)
         near_x = both[:, span:].reshape(ny * tokens, width)
         rows_x = gather(near_x, "gx", nx).reshape(total, width)
 

time: 131 us -> 131 us (level)
  local copies, waits for them, and re-layouts: 4.87 us -> 3.38 us
    unnamed x10 -> x8, local copies, waits for them, and re-layouts: 2.95 us -> 1.33 us
  transfers between devices with their start and end apart: 2 -> 2, of which waited for: 2 -> 2; matrix products, arithmetic and copies ran while one was open for 7% -> 8% of each run, Pallas kernels for 0% -> 0%
where the time goes in v6:
time: 131 us
  blocking collectives  89.4 us (68%)
  waiting for transfers between devices  15.7 us (12%)
  matrix products  9.67 us (7%)
  starting transfers between devices  9.45 us (7%)
  local copies, waits for them, and re-layouts  3.38 us (3%)
  other arithmetic  2.31 us (2%)
    all_to_all x3, blocking collectives, swap(): return lax.all_to_all(blocks, axis, split_axis=0, concat_axis=0, tiled=True)  61.8 us
    all_gather x1, blocking collectives, on_device(): lax.all_gather(jnp.concatenate([mine.astype(jnp.bfloat16), preact]), 'gh'...  22.8 us
    all_to_all x2, waiting for transfers between devices, swap(): return lax.all_to_all(blocks, axis, split_axis=0, concat_axis=0, tiled=True)  15.7 us
    all_to_all x2, starting transfers between devices, swap(): return lax.all_to_all(blocks, axis, split_axis=0, concat_axis=0, tiled=True)  9.45 us
    dot_general x2, matrix products, contract_cols(): lax.dot_general(left, right, (((0,), (0,)), ((), ())), preferred_element_...  5.24 us
    dot_general x2, matrix products, contract_rows(): lax.dot_general(left, right, (((1,), (1,)), ((), ())), preferred_element_...  4.43 us
  transfers between devices with their start and end apart: 2, of which 2 were waited for; matrix products, arithmetic and copies ran while one was open for 8% of the time, Pallas kernels for 0%

profile of v6, /device:TPU:8, one launch (start us, length us, event | category | flops | bytes accessed | tf_op | source)
XLA Modules:
  0.0 130.7 jit_solution(7312638922475832440)
XLA Ops:
  0.6 0.9 pad_maximum_fusion.3
  1.5 20.6 %all_to_all.25 = bf16[8,8,1536]{2,1,0:T(8,128)(2,1)S(1)} all-to-all(bf16[8,8,1536]{2,1,0:T(8,128)(2,1)S(1)} %broadcast_in_dim.21), channel_id=1, replica_groups=mesh['gx'=8,'gy'=8,'gh'=4,'gc'=2] {'gx'}, dimensions={0} | all-to-all | bytes 393216 | tf_op jit(solution)/shard_map/all_to_all | solution.py:34
  22.1 0.1 broadcast_in_dim.22
  22.3 25.9 %all_to_all.26 = bf16[8,72,1536]{2,1,0:T(8,128)(2,1)S(1)} all-to-all(bf16[8,72,1536]{2,1,0:T(8,128)(2,1)S(1)} %broadcast_in_dim.22), channel_id=1, replica_groups=mesh['gx'=8,'gy'=8,'gh'=4,'gc'=2] {'gy'}, dimensions={0} | all-to-all | bytes 3538944 | tf_op jit(solution)/shard_map/all_to_all | solution.py:34
  48.1 0.1 slice.133
  48.3 1.4 %broadcast_in_dim.24 = bf16[8,64,1536]{2,1,0:T(8,128)(2,1)} broadcast(bf16[64,1536]{1,0:T(8,128)(2,1)S(1)} %slice_bitcast_fusion.3), dimensions={1,2} | broadcast | bytes 1769472 | tf_op jit(solution)/shard_map/broadcast_in_dim | solution.py:38
  49.7 4.3 %all-to-all-start.3 = ((bf16[8,64,1536]{2,1,0:T(8,128)(2,1)}), bf16[8,64,1536]{2,1,0:T(8,128)(2,1)}, u32[]{:S(2)}, u32[]{:S(2)}) async-start(bf16[8,64,1536]{2,1,0:T(8,128)(2,1)} %broadcast_in_dim.24), calls=%async_computation.3 | async-start | bytes 3145728 | tf_op jit(solution)/shard_map/all_to_all | solution.py:34
  54.0 2.3 %convolution_bitcast_fusion = f32[2,4,8,8,384]{4,3,0,1,2:T(8,128)S(1)} fusion(bf16[8,4,2,8,1536]{4,3,2,1,0:T(8,128)(2,1)S(1)} %bitcast.60, bf16[384,1536]{1,0:T(8,128)(2,1)} %param.9), kind=kOutput, calls=%fused_computation.3 | convolution fusion | flops 603979776 | bytes 3538944 | tf_op jit(solution)/shard_map/dot_general | solution.py:22
  56.3 0.1 slice_select_fusion.2
  56.4 2.4 %all_gather.16 = f32[2,256,384]{2,1,0:T(8,128)S(1)} all-gather(f32[1,256,384]{2,1,0:T(8,128)S(1)} %bitcast.63), channel_id=1, replica_groups=mesh['gx'=8,'gy'=8,'gh'=4,'gc'=2] {'gc'}, dimensions={0}, use_global_device_ids=true | all-gather | bytes 1179648 | tf_op jit(solution)/shard_map/all_gather | solution.py:74
  58.9 22.8 %all-gather = bf16[1280,384]{1,0:T(8,128)(2,1)S(1)} all-gather(bf16[320,384]{1,0:T(8,128)(2,1)S(1)} %pad_maximum_fusion.1), channel_id=2, replica_groups=mesh['gx'=8,'gy'=8,'gh'=4,'gc'=2] {'gh'}, dimensions={0}, use_global_device_ids=true | all-gather | bytes 1228800 | tf_op jit(solution)/shard_map/all_gather | solution.py:76
  81.8 0.4 fusion.7
  82.2 2.4 %all-gather.1 = bf16[512,768]{1,0:T(8,128)(2,1)S(1)} all-gather(bf16[256,768]{1,0:T(8,128)(2,1)S(1)} %pad_maximum_fusion), channel_id=3, replica_groups=mesh['gx'=8,'gy'=8,'gh'=4,'gc'=2] {'gc'}, dimensions={0}, use_global_device_ids=true | all-gather | bytes 1179648 | tf_op jit(solution)/shard_map/all_gather | solution.py:84
  84.6 0.2 slice_bitcast_fusion
  84.8 2.2 %convolution_convert_fusion = bf16[512,1536]{1,0:T(8,128)(2,1)} fusion(bf16[512,384]{1,0:T(8,128)(2,1)S(1)} %bitcast.62, bf16[1536,384]{1,0:T(8,128)(2,1)S(1)} %copy-done), kind=kOutput, calls=%fused_computation | convolution fusion | flops 604766208 | bytes 3145728 | tf_op jit(solution)/shard_map/dot_general | solution.py:22
  87.0 4.0 %all-to-all-done.3 = bf16[8,64,1536]{2,1,0:T(8,128)(2,1)} async-done(((bf16[8,64,1536]{2,1,0:T(8,128)(2,1)}), bf16[8,64,1536]{2,1,0:T(8,128)(2,1)}, u32[]{:S(2)}, u32[]{:S(2)}) %all-to-all-start.3) | async-done | bytes 1572896 | tf_op jit(solution)/shard_map/all_to_all | solution.py:34
  91.0 5.2 %all-to-all-start.2 = ((bf16[8,64,1536]{2,1,0:T(8,128)(2,1)}), bf16[8,64,1536]{2,1,0:T(8,128)(2,1)S(1)}, u32[]{:S(2)}, u32[]{:S(2)}) async-start(bf16[8,64,1536]{2,1,0:T(8,128)(2,1)} %bitcast.19), calls=%async_computation.2 | async-start | bytes 3145728 | tf_op jit(solution)/shard_map/all_to_all | solution.py:34
  96.3 1.3 %copy-done.2 = bf16[8,64,1536]{2,1,0:T(8,128)(2,1)S(1)} copy-done((bf16[8,64,1536]{2,1,0:T(8,128)(2,1)S(1)}, bf16[8,64,1536]{2,1,0:T(8,128)(2,1)}, u32[]{:S(2)}) %copy-start.2) | copy-done | bytes 1572888
  97.6 1.8 %convolution_convert_fusion.1 = bf16[384,1536]{1,0:T(8,128)(2,1)} fusion(bf16[512,384]{1,0:T(8,128)(2,1)S(1)} %bitcast.65, bf16[512,1536]{1,0:T(8,128)(2,1)S(1)} %bitcast.61), kind=kOutput, calls=%fused_computation.1 | convolution fusion | flops 604569600 | bytes 3145728 | tf_op jit(solution)/shard_map/dot_general | solution.py:28
  99.4 3.4 %convolution_convert_fusion.2 = bf16[1536,384]{1,0:T(8,128)(2,1)} fusion(bf16[512,1536]{1,0:T(8,128)(2,1)} %bitcast.21, bf16[512,384]{1,0:T(8,128)(2,1)S(1)} %bitcast.66), kind=kOutput, calls=%fused_computation.2 | convolution fusion | flops 604569600 | bytes 3145728 | tf_op jit(solution)/shard_map/dot_general | solution.py:28
  102.8 11.7 %all-to-all-done.2 = bf16[8,64,1536]{2,1,0:T(8,128)(2,1)S(1)} async-done(((bf16[8,64,1536]{2,1,0:T(8,128)(2,1)}), bf16[8,64,1536]{2,1,0:T(8,128)(2,1)S(1)}, u32[]{:S(2)}, u32[]{:S(2)}) %all-to-all-start.2) | async-done | bytes 1572896 | tf_op jit(solution)/shard_map/all_to_all | solution.py:34
  114.5 0.2 fusion.15
  114.7 15.4 %all_to_all.27 = bf16[8,8,1536]{2,1,0:T(8,128)(2,1)S(1)} all-to-all(bf16[8,8,1536]{2,1,0:T(8,128)(2,1)S(1)} %fusion.15), channel_id=1, replica_groups=mesh['gx'=8,'gy'=8,'gh'=4,'gc'=2] {'gx'}, dimensions={0} | all-to-all | bytes 393216 | tf_op jit(solution)/shard_map/all_to_all | solution.py:34
  130.1 0.6 fusion.16
  (20 shorter events, 0.4 us)
Async XLA Ops:
  0.6 84.2 %copy-start = (bf16[1536,384]{1,0:T(8,128)(2,1)S(1)}, bf16[1536,384]{1,0:T(8,128)(2,1)}, u32[]{:S(2)}) copy-start(bf16[1536,384]{1,0:T(8,128)(2,1)} %param.8) | copy-start | bytes 3538948
  48.3 5.7 %copy-start.1 = (bf16[8,64,1536]{2,1,0:T(8,128)(2,1)}, bf16[8,64,1536]{2,1,0:T(8,128)(2,1)S(1)}, u32[]{:S(2)}) copy-start(bf16[8,64,1536]{2,1,0:T(8,128)(2,1)S(1)} %slice.133) | copy-start | bytes 4718596
  49.7 41.3 %all-to-all-start.3 = ((bf16[8,64,1536]{2,1,0:T(8,128)(2,1)}), bf16[8,64,1536]{2,1,0:T(8,128)(2,1)}, u32[]{:S(2)}, u32[]{:S(2)}) async-start(bf16[8,64,1536]{2,1,0:T(8,128)(2,1)} %broadcast_in_dim.24), calls=%async_computation.3 | async-start | bytes 3145728 | tf_op jit(solution)/shard_map/all_to_all | solution.py:34
  56.4 2.5 %copy-start.3 = (bf16[64,384]{1,0:T(8,128)(2,1)S(1)}, bf16[64,384]{1,0:T(8,128)(2,1)}, u32[]{:S(2)}) copy-start(bf16[64,384]{1,0:T(8,128)(2,1)} %param.7) | copy-start | bytes 147460
  91.0 23.5 %all-to-all-start.2 = ((bf16[8,64,1536]{2,1,0:T(8,128)(2,1)}), bf16[8,64,1536]{2,1,0:T(8,128)(2,1)S(1)}, u32[]{:S(2)}, u32[]{:S(2)}) async-start(bf16[8,64,1536]{2,1,0:T(8,128)(2,1)} %bitcast.19), calls=%async_computation.2 | async-start | bytes 3145728 | tf_op jit(solution)/shard_map/all_to_all | solution.py:34
  96.2 1.4 %copy-start.2 = (bf16[8,64,1536]{2,1,0:T(8,128)(2,1)S(1)}, bf16[8,64,1536]{2,1,0:T(8,128)(2,1)}, u32[]{:S(2)}) copy-start(bf16[8,64,1536]{2,1,0:T(8,128)(2,1)} %copy-done.1) | copy-start | bytes 4718596

commit v7 on v6

--- a/solution.py
+++ b/solution.py
@@ -79,12 +79,10 @@
         grad_hidden = add_up(chips[:, : nh * rows_z])
         pre = chips[:, nh * rows_z :].reshape(nh * rows_z, hidden_width)
 
-        value, slope = gelu_parts(pre.astype(jnp.float32))
+        _, slope = gelu_parts(pre.astype(jnp.float32))
         grad_pre = (grad_hidden * slope).astype(jnp.bfloat16)
-        pair = lax.all_gather(
-            jnp.concatenate([grad_pre, value.astype(jnp.bfloat16)], axis=1), "gc", axis=0
-        )
-        pair = pair.reshape(nc, nh, ny, tokens, 2 * hidden_width)
+        grad_all = lax.all_gather(grad_pre, "gc", axis=0)
+        grad_all = grad_all.reshape(nc, nh, ny, tokens, hidden_width)
 
         def by_gx(block):
             return block.transpose(1, 0, 2, 3, 4).reshape(total, hidden_width)
@@ -92,9 +90,11 @@
         def by_gy(block):
             return block.transpose(2, 1, 0, 3, 4).reshape(total, hidden_width)
 
-        grad_all, hidden_all = pair[..., :hidden_width], pair[..., hidden_width:]
-
         part_in = contract_rows(by_gy(grad_all), w_in).astype(jnp.bfloat16)
+        part_in, pre = lax.optimization_barrier((part_in, pre))
+        value, _ = gelu_parts(pre.astype(jnp.float32))
+        hidden_all = lax.all_gather(value.astype(jnp.bfloat16), "gc", axis=0)
+        hidden_all = hidden_all.reshape(nc, nh, ny, tokens, hidden_width)
         part_in = swap(part_in.reshape(ny, span, width), "gy")
         grad_w_in = contract_cols(rows_x, by_gx(grad_all)).astype(jnp.bfloat16)
         grad_w_out = contract_cols(by_gy(hidden_all), rows_dy).astype(jnp.bfloat16)

time: 131 us -> 131 us (level)
  local copies, waits for them, and re-layouts: 3.38 us -> 1.88 us
    all_gather x1 -> x2, blocking collectives: 2.37 us -> 4.31 us  [the longest x1 2.22 us: on_device(): hidden_all = lax.all_gather(value.astype(jnp.bfloat16), 'gc', axis=0)]
where the time goes in v7:
time: 131 us; the launch traced here: 130 us
  blocking collectives  90.7 us (69%)
  waiting for transfers between devices  15.1 us (12%)
  matrix products  9.68 us (7%)
  starting transfers between devices  9.46 us (7%)
  other arithmetic  2.38 us (2%)
  local copies, waits for them, and re-layouts  1.88 us (1%)
    all_to_all x3, blocking collectives, swap(): return lax.all_to_all(blocks, axis, split_axis=0, concat_axis=0, tiled=True)  61.2 us
    all_gather x1, blocking collectives, on_device(): lax.all_gather(jnp.concatenate([mine.astype(jnp.bfloat16), preact]), 'gh'...  22.8 us
    all_to_all x2, waiting for transfers between devices, swap(): return lax.all_to_all(blocks, axis, split_axis=0, concat_axis=0, tiled=True)  15.1 us
    all_to_all x2, starting transfers between devices, swap(): return lax.all_to_all(blocks, axis, split_axis=0, concat_axis=0, tiled=True)  9.46 us
    dot_general x2, matrix products, contract_cols(): lax.dot_general(left, right, (((0,), (0,)), ((), ())), preferred_element_...  5.25 us
    dot_general x2, matrix products, contract_rows(): lax.dot_general(left, right, (((1,), (1,)), ((), ())), preferred_element_...  4.43 us
  transfers between devices with their start and end apart: 2, of which 2 were waited for; matrix products, arithmetic and copies ran while one was open for 8% of the time, Pallas kernels for 0%

profile of v7, /device:TPU:8, one launch (start us, length us, event | category | flops | bytes accessed | tf_op | source)
XLA Modules:
  0.0 130.0 jit_solution(14488598967718285543)
XLA Ops:
  0.7 0.9 pad_maximum_fusion.2
  1.5 20.6 %all_to_all.25 = bf16[8,8,1536]{2,1,0:T(8,128)(2,1)S(1)} all-to-all(bf16[8,8,1536]{2,1,0:T(8,128)(2,1)S(1)} %broadcast_in_dim.21), channel_id=1, replica_groups=mesh['gx'=8,'gy'=8,'gh'=4,'gc'=2] {'gx'}, dimensions={0} | all-to-all | bytes 393216 | tf_op jit(solution)/shard_map/all_to_all | solution.py:34
  22.1 0.1 broadcast_in_dim.22
  22.3 25.9 %all_to_all.26 = bf16[8,72,1536]{2,1,0:T(8,128)(2,1)S(1)} all-to-all(bf16[8,72,1536]{2,1,0:T(8,128)(2,1)S(1)} %broadcast_in_dim.22), channel_id=1, replica_groups=mesh['gx'=8,'gy'=8,'gh'=4,'gc'=2] {'gy'}, dimensions={0} | all-to-all | bytes 3538944 | tf_op jit(solution)/shard_map/all_to_all | solution.py:34
  48.1 0.1 slice.125
  48.3 1.4 %broadcast_in_dim.24 = bf16[8,64,1536]{2,1,0:T(8,128)(2,1)} broadcast(bf16[64,1536]{1,0:T(8,128)(2,1)S(1)} %slice_bitcast_fusion), dimensions={1,2} | broadcast | bytes 1769472 | tf_op jit(solution)/shard_map/broadcast_in_dim | solution.py:38
  49.7 4.3 %all-to-all-start.3 = ((bf16[8,64,1536]{2,1,0:T(8,128)(2,1)}), bf16[8,64,1536]{2,1,0:T(8,128)(2,1)}, u32[]{:S(2)}, u32[]{:S(2)}) async-start(bf16[8,64,1536]{2,1,0:T(8,128)(2,1)} %broadcast_in_dim.24), calls=%async_computation.3 | async-start | bytes 3145728 | tf_op jit(solution)/shard_map/all_to_all | solution.py:34
  54.0 2.3 %convolution_bitcast_fusion = f32[2,4,8,8,384]{4,3,0,1,2:T(8,128)S(1)} fusion(bf16[8,4,2,8,1536]{4,3,2,1,0:T(8,128)(2,1)S(1)} %bitcast.63, bf16[384,1536]{1,0:T(8,128)(2,1)} %param.9), kind=kOutput, calls=%fused_computation.3 | convolution fusion | flops 603979776 | bytes 3538944 | tf_op jit(solution)/shard_map/dot_general | solution.py:22
  56.3 0.1 slice_select_fusion.2
  56.4 2.4 %all_gather.20 = f32[2,256,384]{2,1,0:T(8,128)S(1)} all-gather(f32[1,256,384]{2,1,0:T(8,128)S(1)} %bitcast.67), channel_id=1, replica_groups=mesh['gx'=8,'gy'=8,'gh'=4,'gc'=2] {'gc'}, dimensions={0}, use_global_device_ids=true | all-gather | bytes 1179648 | tf_op jit(solution)/shard_map/all_gather | solution.py:74
  58.9 22.8 %all-gather = bf16[1280,384]{1,0:T(8,128)(2,1)S(1)} all-gather(bf16[320,384]{1,0:T(8,128)(2,1)S(1)} %pad_maximum_fusion), channel_id=2, replica_groups=mesh['gx'=8,'gy'=8,'gh'=4,'gc'=2] {'gh'}, dimensions={0}, use_global_device_ids=true | all-gather | bytes 1228800 | tf_op jit(solution)/shard_map/all_gather | solution.py:76
  81.8 0.4 fusion.13
  82.1 2.1 %all_gather.23 = bf16[2,256,384]{2,1,0:T(8,128)(2,1)S(1)} all-gather(bf16[1,256,384]{2,1,0:T(8,128)(2,1)S(1)} %fusion.13), channel_id=1, replica_groups=mesh['gx'=8,'gy'=8,'gh'=4,'gc'=2] {'gc'}, dimensions={0}, use_global_device_ids=true | all-gather | bytes 589824 | tf_op jit(solution)/shard_map/all_gather | solution.py:84
  84.3 2.2 %convolution_convert_fusion = bf16[512,1536]{1,0:T(8,128)(2,1)} fusion(bf16[512,384]{1,0:T(8,128)(2,1)S(1)} %bitcast.66, bf16[1536,384]{1,0:T(8,128)(2,1)S(1)} %copy-done), kind=kOutput, calls=%fused_computation | convolution fusion | flops 604766208 | bytes 3145728 | tf_op jit(solution)/shard_map/dot_general | solution.py:22
  86.5 4.5 %all-to-all-done.3 = bf16[8,64,1536]{2,1,0:T(8,128)(2,1)} async-done(((bf16[8,64,1536]{2,1,0:T(8,128)(2,1)}), bf16[8,64,1536]{2,1,0:T(8,128)(2,1)}, u32[]{:S(2)}, u32[]{:S(2)}) %all-to-all-start.3) | async-done | bytes 1572896 | tf_op jit(solution)/shard_map/all_to_all | solution.py:34
  91.0 5.2 %all-to-all-start.2 = ((bf16[8,64,1536]{2,1,0:T(8,128)(2,1)}), bf16[8,64,1536]{2,1,0:T(8,128)(2,1)S(1)}, u32[]{:S(2)}, u32[]{:S(2)}) async-start(bf16[8,64,1536]{2,1,0:T(8,128)(2,1)} %bitcast.19), calls=%async_computation.2 | async-start | bytes 3145728 | tf_op jit(solution)/shard_map/all_to_all | solution.py:34
  96.2 0.1 fusion.2
  96.4 2.2 %all-gather.1 = bf16[512,384]{1,0:T(8,128)(2,1)S(1)} all-gather(bf16[256,384]{1,0:T(8,128)(2,1)S(1)} %fusion.2), channel_id=3, replica_groups=mesh['gx'=8,'gy'=8,'gh'=4,'gc'=2] {'gc'}, dimensions={0}, use_global_device_ids=true | all-gather | bytes 589824 | tf_op jit(solution)/shard_map/all_gather | solution.py:96
  98.6 1.8 %convolution_convert_fusion.1 = bf16[384,1536]{1,0:T(8,128)(2,1)} fusion(bf16[512,384]{1,0:T(8,128)(2,1)S(1)} %bitcast.70, bf16[512,1536]{1,0:T(8,128)(2,1)S(1)} %bitcast.64), kind=kOutput, calls=%fused_computation.1 | convolution fusion | flops 604569600 | bytes 3145728 | tf_op jit(solution)/shard_map/dot_general | solution.py:28
  100.5 3.4 %convolution_convert_fusion.2 = bf16[1536,384]{1,0:T(8,128)(2,1)} fusion(bf16[512,1536]{1,0:T(8,128)(2,1)} %bitcast.21, bf16[512,384]{1,0:T(8,128)(2,1)S(1)} %bitcast.69), kind=kOutput, calls=%fused_computation.2 | convolution fusion | flops 604569600 | bytes 3145728 | tf_op jit(solution)/shard_map/dot_general | solution.py:28
  103.9 10.5 %all-to-all-done.2 = bf16[8,64,1536]{2,1,0:T(8,128)(2,1)S(1)} async-done(((bf16[8,64,1536]{2,1,0:T(8,128)(2,1)}), bf16[8,64,1536]{2,1,0:T(8,128)(2,1)S(1)}, u32[]{:S(2)}, u32[]{:S(2)}) %all-to-all-start.2) | async-done | bytes 1572896 | tf_op jit(solution)/shard_map/all_to_all | solution.py:34
  114.4 0.2 fusion.18
  114.6 14.8 %all_to_all.27 = bf16[8,8,1536]{2,1,0:T(8,128)(2,1)S(1)} all-to-all(bf16[8,8,1536]{2,1,0:T(8,128)(2,1)S(1)} %fusion.18), channel_id=1, replica_groups=mesh['gx'=8,'gy'=8,'gh'=4,'gc'=2] {'gx'}, dimensions={0} | all-to-all | bytes 393216 | tf_op jit(solution)/shard_map/all_to_all | solution.py:34
  129.4 0.6 fusion.19
  (20 shorter events, 0.4 us)
Async XLA Ops:
  0.6 83.6 %copy-start = (bf16[1536,384]{1,0:T(8,128)(2,1)S(1)}, bf16[1536,384]{1,0:T(8,128)(2,1)}, u32[]{:S(2)}) copy-start(bf16[1536,384]{1,0:T(8,128)(2,1)} %param.8) | copy-start | bytes 3538948
  48.3 5.7 %copy-start.1 = (bf16[8,64,1536]{2,1,0:T(8,128)(2,1)}, bf16[8,64,1536]{2,1,0:T(8,128)(2,1)S(1)}, u32[]{:S(2)}) copy-start(bf16[8,64,1536]{2,1,0:T(8,128)(2,1)S(1)} %slice.125) | copy-start | bytes 4718596
  49.7 41.3 %all-to-all-start.3 = ((bf16[8,64,1536]{2,1,0:T(8,128)(2,1)}), bf16[8,64,1536]{2,1,0:T(8,128)(2,1)}, u32[]{:S(2)}, u32[]{:S(2)}) async-start(bf16[8,64,1536]{2,1,0:T(8,128)(2,1)} %broadcast_in_dim.24), calls=%async_computation.3 | async-start | bytes 3145728 | tf_op jit(solution)/shard_map/all_to_all | solution.py:34
  56.4 2.5 %copy-start.3 = (bf16[64,384]{1,0:T(8,128)(2,1)S(1)}, bf16[64,384]{1,0:T(8,128)(2,1)}, u32[]{:S(2)}) copy-start(bf16[64,384]{1,0:T(8,128)(2,1)} %param.7) | copy-start | bytes 147460
  91.0 23.4 %all-to-all-start.2 = ((bf16[8,64,1536]{2,1,0:T(8,128)(2,1)}), bf16[8,64,1536]{2,1,0:T(8,128)(2,1)S(1)}, u32[]{:S(2)}, u32[]{:S(2)}) async-start(bf16[8,64,1536]{2,1,0:T(8,128)(2,1)} %bitcast.19), calls=%async_computation.2 | async-start | bytes 3145728 | tf_op jit(solution)/shard_map/all_to_all | solution.py:34
  96.2 2.5 %copy-start.2 = (bf16[8,64,1536]{2,1,0:T(8,128)(2,1)S(1)}, bf16[8,64,1536]{2,1,0:T(8,128)(2,1)}, u32[]{:S(2)}) copy-start(bf16[8,64,1536]{2,1,0:T(8,128)(2,1)} %copy-done.1) | copy-start | bytes 4718596
